TPU v7x, 512 devices: a whole 4x8x8 slice. The times are simulated.
512 devices in a mesh: seq: 128 (over z, y, core), rep: 4 (over x).
Axes of the slice: x: 4, y: 8, z: 8, core: 2. Of those that a mesh axis runs over, the one named last changes fastest.
Arguments:
- tokens: bfloat16 [16384, 2048], P('seq'), may hold values from -6 to 6
- norm_gain: float32 [2048], replicated, may hold values from 0.25 to 1.75
- refusal_dir: float32 [2048], replicated, may hold values from -6 to 6
- expert_ids: int32 [16384, 8], P('seq'), may hold values from 0 to 127, as said below
- gate_probs: float32 [16384, 8], P('seq'), may hold values from 0.05 to 0.5
- w_gate: bfloat16 [128, 768, 2048], P('seq', 'rep'), may hold values from -0.125 to 0.125
- w_up: bfloat16 [128, 768, 2048], P('seq', 'rep'), may hold values from -0.125 to 0.125
- w_down: bfloat16 [128, 768, 2048], P('seq', 'rep'), may hold values from -0.21875 to 0.21875
Outputs:
- ablated: bfloat16 [16384, 2048], P('seq', 'rep')
Inputs may be any that keep to these rules, and one draw needn't show every extreme that they name: `expert_ids`: each row names 8 different experts. Among the 128 rows of one device no expert is named more than 12 times, and some expert is named exactly 12 times in the rows of every device.
All inputs are finite; a program needn't handle non-finite values.
Results may differ from a plain program's by a relative error of at most 0.0095.
Values may be sent and summed in bfloat16 or wider, within the bound.
A program may use at most 128 MiB of HBM per device.

v0:
```python
import jax
import jax.numpy as jnp
from jax import lax
from jax.sharding import PartitionSpec as P

CAP = 12


def local(tokens, norm_gain, refusal_dir, expert_ids, gate_probs, w_gate, w_up, w_down):
    tok_rows, model_width = tokens.shape
    top_k = expert_ids.shape[1]
    n_seq = lax.axis_size("seq")
    n_rep = lax.axis_size("rep")
    exp_dev = w_gate.shape[0]
    experts = exp_dev * n_seq
    slot_count = tok_rows * top_k
    part_width = model_width // n_rep
    tokens_f32 = tokens.astype(jnp.float32)
    inv_rms = lax.rsqrt(jnp.mean(tokens_f32 * tokens_f32, axis=1, keepdims=True) + 1e-06)
    normed = (tokens_f32 * inv_rms * norm_gain).astype(jnp.bfloat16)
    flat_ids = expert_ids.reshape(slot_count)
    onehot = (flat_ids[:, None] == jnp.arange(experts, dtype=jnp.int32)[None, :]).astype(jnp.int32)
    slot_rank = jnp.sum(jnp.cumsum(onehot, axis=0) * onehot, axis=1) - 1
    target = flat_ids * CAP + slot_rank
    repeated = jnp.broadcast_to(normed[:, None, :], (tok_rows, top_k, model_width)).reshape(
        slot_count, model_width
    )
    sendbuf = jnp.zeros((experts * CAP, model_width), jnp.bfloat16).at[target].set(repeated)
    sendbuf = sendbuf.reshape(n_seq, exp_dev, CAP, model_width)
    arrived = lax.all_to_all(sendbuf, "seq", split_axis=0, concat_axis=0, tiled=True)
    gate_val = jnp.einsum("secd,efd->secf", arrived, w_gate, preferred_element_type=jnp.float32)
    up_val = jnp.einsum("secd,efd->secf", arrived, w_up, preferred_element_type=jnp.float32)
    hidden = (jax.nn.silu(gate_val) * up_val).astype(jnp.bfloat16)
    pieces = jnp.einsum(
        "secf,efd->secd", hidden, w_down, preferred_element_type=jnp.float32
    ).astype(jnp.bfloat16)
    probs_flat = gate_probs.reshape(slot_count)[:, None]
    returned = lax.all_to_all(pieces, "seq", split_axis=0, concat_axis=0, tiled=True)
    returned = returned.reshape(experts * CAP, model_width)
    weighted = returned[target].astype(jnp.float32) * probs_flat
    moe_part = jnp.sum(weighted.reshape(tok_rows, top_k, model_width), axis=1)
    summed = lax.psum_scatter(
        moe_part.astype(jnp.bfloat16), "rep", scatter_dimension=1, tiled=True
    ).astype(jnp.float32)
    unit_dir = refusal_dir / jnp.sqrt(jnp.sum(refusal_dir * refusal_dir) + 1e-06)
    rep_offset = lax.axis_index("rep") * part_width
    unit_slice = lax.dynamic_slice_in_dim(unit_dir, rep_offset, part_width, 0)
    own_tokens = lax.dynamic_slice_in_dim(tokens_f32, rep_offset, part_width, 1)
    residual = own_tokens + summed
    along_dir = lax.psum(jnp.sum(residual * unit_slice, axis=1), "rep")
    return (residual - along_dir[:, None] * unit_slice).astype(jnp.bfloat16)


def solution(mesh):
    placed = (
        P("seq", None),
        P(),
        P(),
        P("seq", None),
        P("seq", None),
        P("seq", "rep", None),
        P("seq", "rep", None),
        P("seq", "rep", None),
    )
    return jax.shard_map(
        local, mesh=mesh, in_specs=placed, out_specs=P("seq", "rep"), check_vma=False
    )
```

profile of v0, /device:TPU:1, one launch (start us, length us, event | category | flops | bytes accessed | tf_op | source)
XLA Modules:
  0.0 618.3 jit_solution(5903693957242222110)
XLA Ops:
  6.5 0.9 copy.19
  7.4 0.1 eq.29
  7.5 0.1 eq.25
  7.6 0.7 broadcast_multiply_fusion
  8.3 0.1 copy.21
  8.4 0.2 fusion.34
  8.7 0.1 copy.22
  8.8 0.4 fusion.33
  9.2 0.1 copy.18
  9.3 0.1 mul.82
  9.4 1.2 multiply_reduce_fusion
  10.6 1.2 multiply_convert_fusion
  11.9 10.3 %scatter_custom_fusion = bf16[1536,2048]{1,0:T(8,128)(2,1)} fusion(s32[1024]{0:T(1024)S(1)} %bitcast.78, bf16[]{:T(256)} %constant.16.clone.1, bf16[128,2048]{1,0:T(8,128)(2,1)S(1)} %multiply_convert_fusion), kind=kCustom, calls=%fused_computation.11 | custom fusion | bytes 6815746 | tf_op jit(solution)/shard_map/scatter | solution.py:28
  22.1 10.6 %reshape.104 = bf16[128,1,12,2048]{3,2,0,1:T(8,128)(2,1)} reshape(bf16[1536,2048]{1,0:T(8,128)(2,1)} %scatter_custom_fusion) | data formatting | bytes 12582912 | tf_op jit(solution)/shard_map/reshape | solution.py:29
  32.7 208.6 %all_to_all.10 = bf16[128,1,12,2048]{3,2,1,0:T(8,128)(2,1)S(1)} all-to-all(bf16[128,1,12,2048]{3,2,1,0:T(8,128)(2,1)} %bitcast.77), channel_id=1, replica_groups=mesh['seq'=128,'rep'=4] {'seq'}, dimensions={0} | all-to-all | bytes 12582912 | tf_op jit(solution)/shard_map/all_to_all | solution.py:30
  241.3 3.3 copy-done.1
  244.6 7.2 %fusion.11 = f32[128,1,12,192]{0,3,2,1:T(8,128)S(1)} fusion(bf16[128,1,12,2048]{3,2,1,0:T(8,128)(2,1)S(1)} %all_to_all.10, bf16[1,192,2048]{2,1,0:T(8,128)(2,1)S(1)} %copy-done.5), kind=kOutput, calls=%fused_computation.15 | convolution fusion | flops 1207959552 | bytes 8257536 | tf_op jit(solution)/shard_map/secd,efd->secf/dot_general | solution.py:31
  251.9 15.3 %convert_bitcast_fusion = bf16[128,1,12,2048]{3,0,2,1:T(8,128)(2,1)} fusion(bf16[128,1,12,2048]{3,2,1,0:T(8,128)(2,1)} %copy-done.1, f32[128,1,12,192]{0,3,2,1:T(8,128)S(1)} %fusion.11, bf16[1,192,2048]{2,1,0:T(8,128)(2,1)S(1)} %copy-done, bf16[1,192,2048]{2,1,0:T(8,128)(2,1)S(1)} %copy-done.6), kind=kOutput, calls=%fused_computation.8 | convolution fusion | flops 2420834304 | bytes 15335424 | tf_op jit(solution)/shard_map/secf,efd->secd/dot_general | solution.py:34
  267.2 9.6 %copy.25 = bf16[128,1,12,2048]{3,2,1,0:T(8,128)(2,1)} copy(bf16[128,1,12,2048]{3,0,2,1:T(8,128)(2,1)} %convert_bitcast_fusion) | data formatting | bytes 12582912 | tf_op jit(solution)/shard_map/convert_element_type | solution.py:36
  276.8 19.8 %all-to-all-start.1 = ((bf16[128,1,12,2048]{3,2,1,0:T(8,128)(2,1)}), bf16[128,1,12,2048]{3,2,1,0:T(8,128)(2,1)}, u32[]{:S(2)}, u32[]{:S(2)}) async-start(bf16[128,1,12,2048]{3,2,1,0:T(8,128)(2,1)} %copy.25), calls=%async_computation.1 | async-start | bytes 16777216 | tf_op jit(solution)/shard_map/all_to_all | solution.py:38
  296.7 0.1 copy.26
  296.8 223.4 %all-to-all-done.1 = bf16[128,1,12,2048]{3,2,1,0:T(8,128)(2,1)} async-done(((bf16[128,1,12,2048]{3,2,1,0:T(8,128)(2,1)}), bf16[128,1,12,2048]{3,2,1,0:T(8,128)(2,1)}, u32[]{:S(2)}, u32[]{:S(2)}) %all-to-all-start.1) | async-done | bytes 6291488 | tf_op jit(solution)/shard_map/all_to_all | solution.py:38
  520.2 10.9 %reshape.110 = bf16[1536,2048]{1,0:T(8,128)(2,1)} reshape(bf16[128,1,12,2048]{3,2,1,0:T(8,128)(2,1)} %all-to-all-done.1) | data formatting | bytes 12582912 | tf_op jit(solution)/shard_map/reshape | solution.py:39
  531.1 12.5 %gather_fusion = bf16[1024,2048]{1,0:T(8,128)(2,1)} fusion(bf16[1536,2048]{1,0:T(8,128)(2,1)} %reshape.110, s32[1024]{0:T(1024)S(1)} %broadcast_clamp_fusion), kind=kCustom, calls=%fused_computation | custom fusion | bytes 8392704 | tf_op jit(solution)/shard_map/gather | solution.py:40
  543.6 7.3 %fusion = bf16[128,2048]{1,0:T(8,128)(2,1)} fusion(bf16[1024,2048]{1,0:T(8,128)(2,1)} %gather_fusion, f32[128,8]{1,0:T(8,128)S(1)} %copy.26), kind=kLoop, calls=%fused_computation.3 | loop fusion | flops 6029312 | bytes 4722688 | tf_op jit(solution)/shard_map/reduce_sum | solution.py:41
  551.0 0.1 convert_element_type.42
  551.1 0.6 multiply_reduce_fusion.2
  552.4 0.1 dynamic-slice_divide_fusion
  552.5 49.8 %reduce-scatter.2.cloned.1.call-done = bf16[128,512]{1,0:T(8,128)(2,1)} async-done(((bf16[128,2048]{1,0:T(8,128)(2,1)}), bf16[128,512]{1,0:T(8,128)(2,1)}) %reduce-scatter.2.cloned.1.call-update) | async-done | bytes 131088 | tf_op jit(solution)/shard_map/reduce_scatter | solution.py:42
  602.3 1.0 multiply_reduce_fusion.1
  603.3 6.1 psum.7
  609.4 1.6 subtract_convert_fusion
  (23 shorter events, 0.2 us)
Async XLA Ops:
  6.5 245.3 %copy-start = (bf16[1,192,2048]{2,1,0:T(8,128)(2,1)S(1)}, bf16[1,192,2048]{2,1,0:T(8,128)(2,1)}, u32[]{:S(2)}) copy-start(bf16[1,192,2048]{2,1,0:T(8,128)(2,1)} %param.15) | copy-start | bytes 2359300
  32.7 211.9 %copy-start.5 = (bf16[1,192,2048]{2,1,0:T(8,128)(2,1)S(1)}, bf16[1,192,2048]{2,1,0:T(8,128)(2,1)}, u32[]{:S(2)}) copy-start(bf16[1,192,2048]{2,1,0:T(8,128)(2,1)} %param.13) | copy-start | bytes 2359300
  241.3 3.3 copy-start.1
  244.6 7.2 %copy-start.6 = (bf16[1,192,2048]{2,1,0:T(8,128)(2,1)S(1)}, bf16[1,192,2048]{2,1,0:T(8,128)(2,1)}, u32[]{:S(2)}) copy-start(bf16[1,192,2048]{2,1,0:T(8,128)(2,1)} %param.14) | copy-start | bytes 2359300
  276.8 19.9 %copy-start.4 = (f32[128,8]{0,1:T(8,128)S(1)}, f32[128,8]{0,1:T(8,128)}, u32[]{:S(2)}) copy-start(f32[128,8]{0,1:T(8,128)} %param.12) | copy-start | bytes 12292
  276.8 243.4 %all-to-all-start.1 = ((bf16[128,1,12,2048]{3,2,1,0:T(8,128)(2,1)}), bf16[128,1,12,2048]{3,2,1,0:T(8,128)(2,1)}, u32[]{:S(2)}, u32[]{:S(2)}) async-start(bf16[128,1,12,2048]{3,2,1,0:T(8,128)(2,1)} %copy.25), calls=%async_computation.1 | async-start | bytes 16777216 | tf_op jit(solution)/shard_map/all_to_all | solution.py:38
  296.6 305.7 %reduce-scatter.2.cloned.1.call-start = ((), (), s32[]{:S(2)}) async-start(), calls=%async_computation.3 | async-start | bytes 655360 | tf_op jit(solution)/shard_map/reduce_scatter | solution.py:42
  531.1 19.8 %copy-start.2 = (bf16[128,2048]{1,0:T(8,128)(2,1)S(1)}, bf16[128,2048]{1,0:T(8,128)(2,1)}, u32[]{:S(2)}) copy-start(bf16[128,2048]{1,0:T(8,128)(2,1)} %param.8) | copy-start | bytes 1572868
  543.6 7.5 %copy-start.3 = (f32[2048]{0:T(1024)S(1)}, f32[2048]{0:T(1024)}, u32[]{:S(2)}) copy-start(f32[2048]{0:T(1024)} %param.10) | copy-start | bytes 24580
Sparse Core Ops, SparseCore 0:
  551.1 51.1 reduce-scatter.1
where the time goes:
time: 629 us; the launch traced here: 618 us
  waiting for transfers between devices  273 us (43%)
  blocking collectives  215 us (34%)
  local copies, waits for them, and re-layouts  58.8 us (9%)
  matrix products  22.5 us (4%)
  starting transfers between devices  19.8 us (3%)
  between operations  14.7 us (2%)
  other arithmetic  14.6 us (2%)
    all_to_all x1, waiting for transfers between devices, local(): lax.all_to_all(pieces, 'seq', split_axis=0, concat_axis=0, tiled=True)  223 us
    all_to_all x1, blocking collectives, local(): lax.all_to_all(sendbuf, 'seq', split_axis=0, concat_axis=0, tiled=True)  209 us
    reduce_scatter x1, waiting for transfers between devices, local(): lax.psum_scatter(moe_part.astype(jnp.bfloat16), 'rep', scatter_dimension=...  49.8 us
    all_to_all x1, starting transfers between devices, local(): lax.all_to_all(pieces, 'seq', split_axis=0, concat_axis=0, tiled=True)  19.8 us
    dot_general x1, matrix products, local(): jnp.einsum('secf,efd->secd', hidden, w_down, preferred_element_type=jnp.f...  15.3 us
  transfers between devices with their start and end apart: 2, of which 2 were waited for; matrix products, arithmetic and copies ran while one was open for 0% of the time, Pallas kernels for 0%

commit v1 on v0

v1 whole, which is shorter than its diff:
```python
import jax
import jax.numpy as jnp
from jax import lax
from jax.sharding import PartitionSpec as P

CAP = 12


def local(tokens, norm_gain, refusal_dir, expert_ids, gate_probs, w_gate, w_up, w_down):
    tok_rows, model_width = tokens.shape
    n_seq = lax.axis_size("seq")
    n_rep = lax.axis_size("rep")
    slots = CAP // n_rep
    part_width = model_width // n_rep
    rep = lax.axis_index("rep")
    wg = lax.all_gather(w_gate[0], "rep", axis=0, tiled=True)
    wu = lax.all_gather(w_up[0], "rep", axis=0, tiled=True)
    wd = lax.all_gather(w_down[0], "rep", axis=0, tiled=True)
    tokens_f32 = tokens.astype(jnp.float32)
    inv_rms = lax.rsqrt(jnp.mean(tokens_f32 * tokens_f32, axis=1, keepdims=True) + 1e-06)
    normed = (tokens_f32 * inv_rms * norm_gain).astype(jnp.bfloat16)
    same = expert_ids[:, :, None] == jnp.arange(n_seq, dtype=jnp.int32)[None, None, :]
    chosen = jnp.any(same, axis=1)
    probs = jnp.sum(jnp.where(same, gate_probs[:, :, None], 0.0), axis=1)
    order = jnp.arange(tok_rows)
    earlier = (order[:, None] > order[None, :]).astype(jnp.bfloat16)
    rank = jnp.dot(earlier, chosen.astype(jnp.bfloat16), preferred_element_type=jnp.float32)
    rank = rank.astype(jnp.int32) - slots * rep
    picked = jnp.stack([chosen & (rank == c) for c in range(slots)])
    sendbuf = jnp.einsum(
        "cte,td->ecd", picked.astype(jnp.bfloat16), normed, preferred_element_type=jnp.float32
    ).astype(jnp.bfloat16)
    arrived = lax.all_to_all(sendbuf, "seq", split_axis=0, concat_axis=0, tiled=True)
    gate_val = jnp.einsum("scd,fd->scf", arrived, wg, preferred_element_type=jnp.float32)
    up_val = jnp.einsum("scd,fd->scf", arrived, wu, preferred_element_type=jnp.float32)
    hidden = (jax.nn.silu(gate_val) * up_val).astype(jnp.bfloat16)
    pieces = jnp.einsum("scf,fd->scd", hidden, wd, preferred_element_type=jnp.float32).astype(
        jnp.bfloat16
    )
    returned = lax.all_to_all(pieces, "seq", split_axis=0, concat_axis=0, tiled=True)
    weight = jnp.where(picked, probs[None], 0.0)
    high = weight.astype(jnp.bfloat16)
    low = (weight - high.astype(jnp.float32)).astype(jnp.bfloat16)
    both = jnp.concatenate([high, low], axis=1)
    moe = jnp.einsum("cte,ecd->td", both, returned, preferred_element_type=jnp.float32)
    moe = moe[:tok_rows] + moe[tok_rows:]
    unit_dir = refusal_dir / jnp.sqrt(jnp.sum(refusal_dir * refusal_dir) + 1e-06)
    along_dir = jnp.sum(tokens_f32 * unit_dir, axis=1) + lax.psum(
        jnp.sum(moe * unit_dir, axis=1), "rep"
    )
    parts = moe.astype(jnp.bfloat16).reshape(tok_rows, n_rep, part_width).transpose(1, 0, 2)
    parts = lax.all_to_all(parts, "rep", split_axis=0, concat_axis=0, tiled=True)
    summed = jnp.sum(parts.astype(jnp.float32), axis=0)
    rep_offset = rep * part_width
    unit_slice = lax.dynamic_slice_in_dim(unit_dir, rep_offset, part_width, 0)
    own_tokens = lax.dynamic_slice_in_dim(tokens_f32, rep_offset, part_width, 1)
    residual = own_tokens + summed
    return (residual - along_dir[:, None] * unit_slice).astype(jnp.bfloat16)


def solution(mesh):
    placed = (
        P("seq", None),
        P(),
        P(),
        P("seq", None),
        P("seq", None),
        P("seq", "rep", None),
        P("seq", "rep", None),
        P("seq", "rep", None),
    )
    return jax.shard_map(
        local, mesh=mesh, in_specs=placed, out_specs=P("seq", "rep"), check_vma=False
    )
```

time: 629 us -> 261 us (0.41); the launches traced: 618 us -> 257 us
  waiting for transfers between devices: 273 us -> 115 us
  blocking collectives: 215 us -> 79.3 us
  local copies, waits for them, and re-layouts: 58.8 us -> 8.56 us
  other arithmetic: 14.6 us -> 2.68 us
    all_to_all x1, waiting for transfers between devices: 223 us -> 50.7 us  [local(): lax.all_to_all(pieces, 'seq', split_axis=0, concat_axis=0, tiled=True)]
    all_to_all x1, blocking collectives: 209 us -> 69.6 us  [local(): lax.all_to_all(sendbuf, 'seq', split_axis=0, concat_axis=0, tiled=True)]
    all_gather x0 -> x3, waiting for transfers between devices: none -> 62.1 us  [the longest x1 47.3 us: local(): wu = lax.all_gather(w_up[0], 'rep', axis=0, tiled=True)]
    reduce_scatter x1 -> x0, waiting for transfers between devices: 49.8 us -> none  [local(): lax.psum_scatter(moe_part.astype(jnp.bfloat16), 'rep', scatter_dimension=...]
    reshape x2 -> x1, local copies, waits for them, and re-layouts: 21.5 us -> 0.83 us  [local(): moe.astype(jnp.bfloat16).reshape(tok_rows, n_rep, part_width)]
    gather x1 -> x0, local copies, waits for them, and re-layouts: 12.5 us -> none  [local(): weighted = returned[target].astype(jnp.float32) * probs_flat]
    scatter x1 -> x0, local copies, waits for them, and re-layouts: 10.3 us -> none  [local(): jnp.zeros((experts * CAP, model_width), jnp.bfloat16).at[target]]
    reduce_sum x4, other arithmetic: 9.93 us -> 0.88 us  [the longest x1 0.34 us: local(): probs = jnp.sum(jnp.where(same, gate_probs[:, :, None], 0.0), axis=1)]
  transfers between devices with their start and end apart: 2 -> 5, of which waited for: 2 -> 3; matrix products, arithmetic and copies ran while one was open for 0% -> 5% of each run, Pallas kernels for 0% -> 0%
where the time goes in v1:
time: 261 us; the launch traced here: 257 us
  waiting for transfers between devices  115 us (44%)
  blocking collectives  79.3 us (30%)
  matrix products  19.4 us (7%)
  starting transfers between devices  18.2 us (7%)
  between operations  13.9 us (5%)
  local copies, waits for them, and re-layouts  8.56 us (3%)
  other arithmetic  2.68 us (1%)
    all_to_all x1, blocking collectives, local(): lax.all_to_all(sendbuf, 'seq', split_axis=0, concat_axis=0, tiled=True)  69.6 us
    all_to_all x1, waiting for transfers between devices, local(): lax.all_to_all(pieces, 'seq', split_axis=0, concat_axis=0, tiled=True)  50.7 us
    all_gather x1, waiting for transfers between devices, local(): wu = lax.all_gather(w_up[0], 'rep', axis=0, tiled=True)  47.3 us
    all_gather x1, waiting for transfers between devices, local(): wd = lax.all_gather(w_down[0], 'rep', axis=0, tiled=True)  14.8 us
    all_to_all x1, starting transfers between devices, local(): lax.all_to_all(pieces, 'seq', split_axis=0, concat_axis=0, tiled=True)  14.6 us
    psum x1, blocking collectives, local(): lax.psum(jnp.sum(moe * unit_dir, axis=1), 'rep')  9.73 us
    dot_general x1, matrix products, local(): jnp.einsum('scf,fd->scd', hidden, wd, preferred_element_type=jnp.float32)  8.74 us
    dot_general x1, matrix products, local(): jnp.einsum('scd,fd->scf', arrived, wg, preferred_element_type=jnp.float32)  6.58 us
  transfers between devices with their start and end apart: 5, of which 3 were waited for; matrix products, arithmetic and copies ran while one was open for 5% of the time, Pallas kernels for 0%

profile of v1, /device:TPU:1, one launch (start us, length us, event | category | flops | bytes accessed | tf_op | source)
XLA Modules:
  0.0 256.9 jit_solution(1011948597753482893)
XLA Ops:
  6.5 0.0 all-gather.7.cloned.1.call-start
  6.6 0.7 all-gather.7.cloned.1.call-update
  7.3 0.0 all-gather.11.cloned.1.call-start
  7.3 0.7 all-gather.11.cloned.1.call-update
  8.0 0.0 all-gather.9.cloned.1.call-start
  8.1 0.7 all-gather.9.cloned.1.call-update
  8.8 0.1 copy.20
  8.9 0.3 fusion.29
  9.1 0.6 multiply_reduce_fusion.3
  10.5 0.3 multiply_reduce_fusion.1
  10.7 0.2 and_bitcast_fusion.2
  10.9 1.9 fusion.9
  12.8 3.3 %copy.23 = bf16[128,3,2048]{2,1,0:T(4,128)(2,1)S(1)} copy(bf16[128,3,2048]{0,2,1:T(8,128)(2,1)} %fusion.9) | data formatting | bytes 3145728 | tf_op jit(solution)/shard_map/convert_element_type | solution.py:32
  16.1 69.6 %all_to_all.15 = bf16[128,3,2048]{2,1,0:T(4,128)(2,1)} all-to-all(bf16[128,3,2048]{2,1,0:T(4,128)(2,1)S(1)} %copy.23), channel_id=1, replica_groups=mesh['seq'=128,'rep'=4] {'seq'}, dimensions={0} | all-to-all | bytes 3145728 | tf_op jit(solution)/shard_map/all_to_all | solution.py:33
  85.7 6.6 %fusion.4 = f32[128,3,768]{2,0,1:T(8,128)} fusion(bf16[1,768,2048]{2,1,0:T(8,128)(2,1)} %all-gather.7.cloned.1.call-done, bf16[128,3,2048]{2,1,0:T(4,128)(2,1)} %all_to_all.15), kind=kOutput, calls=%fused_computation.4 | convolution fusion | flops 1207959552 | bytes 5898240 | tf_op jit(solution)/shard_map/scd,fd->scf/dot_general | solution.py:34
  92.3 14.8 %all-gather.11.cloned.1.call-done = bf16[1,768,2048]{2,1,0:T(8,128)(2,1)} async-done(((bf16[1,192,2048]{2,1,0:T(8,128)(2,1)}), bf16[1,768,2048]{2,1,0:T(8,128)(2,1)}) %all-gather.11.cloned.1.call-update) | async-done | bytes 3145744 | tf_op jit(solution)/shard_map/all_gather | solution.py:18
  107.1 47.3 %all-gather.9.cloned.1.call-done = bf16[1,768,2048]{2,1,0:T(8,128)(2,1)} async-done(((bf16[1,192,2048]{2,1,0:T(8,128)(2,1)}), bf16[1,768,2048]{2,1,0:T(8,128)(2,1)}) %all-gather.9.cloned.1.call-update) | async-done | bytes 3145744 | tf_op jit(solution)/shard_map/all_gather | solution.py:17
  154.4 8.7 %fusion.6 = bf16[128,3,2048]{2,0,1:T(8,128)(2,1)} fusion(bf16[1,768,2048]{2,1,0:T(8,128)(2,1)} %all-gather.11.cloned.1.call-done, bf16[1,768,2048]{2,1,0:T(8,128)(2,1)} %all-gather.9.cloned.1.call-done, f32[128,3,768]{2,0,1:T(8,128)} %fusion.4, bf16[128,3,2048]{2,1,0:T(4,128)(2,1)S(1)} %copy-done.1), kind=kOutput, calls=%fused_computation.6 | convolution fusion | flops 2418475008 | bytes 10616832 | tf_op jit(solution)/shard_map/scf,fd->scd/dot_general | solution.py:37
  163.1 4.1 %copy.26 = bf16[128,3,2048]{2,1,0:T(4,128)(2,1)} copy(bf16[128,3,2048]{2,0,1:T(8,128)(2,1)} %fusion.6) | data formatting | bytes 3145728 | tf_op jit(solution)/shard_map/convert_element_type | solution.py:37
  167.2 14.6 %all-to-all-start.1 = ((bf16[128,3,2048]{2,1,0:T(4,128)(2,1)}), bf16[128,3,2048]{2,1,0:T(4,128)(2,1)S(1)}, u32[]{:S(2)}, u32[]{:S(2)}) async-start(bf16[128,3,2048]{2,1,0:T(4,128)(2,1)} %copy.26), calls=%async_computation.1 | async-start | bytes 4194304 | tf_op jit(solution)/shard_map/all_to_all | solution.py:40
  181.8 0.1 copy.21
  181.9 0.3 select_reduce_fusion
  182.4 50.7 %all-to-all-done.1 = bf16[128,3,2048]{2,1,0:T(4,128)(2,1)S(1)} async-done(((bf16[128,3,2048]{2,1,0:T(4,128)(2,1)}), bf16[128,3,2048]{2,1,0:T(4,128)(2,1)S(1)}, u32[]{:S(2)}, u32[]{:S(2)}) %all-to-all-start.1) | async-done | bytes 1572896 | tf_op jit(solution)/shard_map/all_to_all | solution.py:40
  233.1 2.0 convolution_bitcast_fusion
  235.1 0.2 multiply_reduce_fusion
  235.3 0.8 copy.41
  236.2 3.5 %all-to-all-start.2 = ((bf16[4,128,512]{2,1,0:T(8,128)(2,1)}), bf16[4,128,512]{2,1,0:T(8,128)(2,1)S(1)}, u32[]{:S(2)}, u32[]{:S(2)}) async-start(bf16[4,128,512]{2,1,0:T(8,128)(2,1)} %bitcast.40), calls=%async_computation.2 | async-start | bytes 1048576 | tf_op jit(solution)/shard_map/all_to_all | solution.py:52
  239.7 0.1 convert_element_type.42
  239.8 0.1 dynamic_slice.7
  239.8 9.7 %psum.7 = f32[128]{0:T(128)S(1)} all-reduce(f32[128]{0:T(128)S(1)} %get-tuple-element.7), channel_id=1, replica_groups=mesh['seq'=128,'rep'=4] {'rep'}, use_global_device_ids=true, to_apply=%region_7.8 | all-reduce | flops 128 | bytes 1024 | tf_op jit(solution)/shard_map/psum | solution.py:48
  249.6 0.1 convert_reduce_fusion
  249.6 0.8 subtract_convert_fusion
  (19 shorter events, 0.1 us)
Async XLA Ops:
  6.5 2.2 copy-start.4
  6.5 2.6 %copy-start.2 = (f32[2048]{0:T(1024)S(1)}, f32[2048]{0:T(1024)}, u32[]{:S(2)}) copy-start(f32[2048]{0:T(1024)} %param.10) | copy-start | bytes 24580
  6.5 3.9 %copy-start = (bf16[128,2048]{1,0:T(8,128)(2,1)S(1)}, bf16[128,2048]{1,0:T(8,128)(2,1)}, u32[]{:S(2)}) copy-start(bf16[128,2048]{1,0:T(8,128)(2,1)} %param.8) | copy-start | bytes 1572868
  6.5 4.4 %copy-start.3 = (f32[2048]{0:T(1024)S(1)}, f32[2048]{0:T(1024)}, u32[]{:S(2)}) copy-start(f32[2048]{0:T(1024)} %param.9) | copy-start | bytes 24580
  6.5 79.2 %all-gather.7.cloned.1.call-start = ((), (), s32[]{:S(2)}) async-start(), calls=%async_computation.3 | async-start | bytes 3932160 | tf_op jit(solution)/shard_map/all_gather | solution.py:16
  7.3 99.8 %all-gather.11.cloned.1.call-start = ((), (), s32[]{:S(2)}) async-start(), calls=%async_computation.5 | async-start | bytes 3932160 | tf_op jit(solution)/shard_map/all_gather | solution.py:18
  8.0 146.3 %all-gather.9.cloned.1.call-start = ((), (), s32[]{:S(2)}) async-start(), calls=%async_computation.4 | async-start | bytes 3932160 | tf_op jit(solution)/shard_map/all_gather | solution.py:17
  85.7 68.7 %copy-start.1 = (bf16[128,3,2048]{2,1,0:T(4,128)(2,1)S(1)}, bf16[128,3,2048]{2,1,0:T(4,128)(2,1)}, u32[]{:S(2)}) copy-start(bf16[128,3,2048]{2,1,0:T(4,128)(2,1)} %all_to_all.15) | copy-start | bytes 4718596
  167.2 14.6 %copy-start.5 = (f32[128,8]{0,1:T(8,128)S(1)}, f32[128,8]{0,1:T(8,128)}, u32[]{:S(2)}) copy-start(f32[128,8]{0,1:T(8,128)} %param.12) | copy-start | bytes 12292
  167.2 65.9 %all-to-all-start.1 = ((bf16[128,3,2048]{2,1,0:T(4,128)(2,1)}), bf16[128,3,2048]{2,1,0:T(4,128)(2,1)S(1)}, u32[]{:S(2)}, u32[]{:S(2)}) async-start(bf16[128,3,2048]{2,1,0:T(4,128)(2,1)} %copy.26), calls=%async_computation.1 | async-start | bytes 4194304 | tf_op jit(solution)/shard_map/all_to_all | solution.py:40
  236.2 13.4 %all-to-all-start.2 = ((bf16[4,128,512]{2,1,0:T(8,128)(2,1)}), bf16[4,128,512]{2,1,0:T(8,128)(2,1)S(1)}, u32[]{:S(2)}, u32[]{:S(2)}) async-start(bf16[4,128,512]{2,1,0:T(8,128)(2,1)} %bitcast.40), calls=%async_computation.2 | async-start | bytes 1048576 | tf_op jit(solution)/shard_map/all_to_all | solution.py:52
Sparse Core Ops, SparseCore 0:
  9.5 50.3 all-gather.6
  62.0 45.1 all-gather.10
  109.2 45.1 all-gather.8

commit v2 on v0

v2 whole, which is shorter than its diff:
```python
import functools

import jax
import jax.numpy as jnp
from jax import lax
from jax.experimental import pallas as pl
from jax.experimental.pallas import tpu as pltpu
from jax.sharding import PartitionSpec as P

CAP = 12
LANES = 128
MESH = pl.DeviceIdType.MESH
F32 = jnp.float32
BF16 = jnp.bfloat16


def dot(a, b, dims):
    return lax.dot_general(a, b, (dims, ((), ())), preferred_element_type=F32)


def kernel(
    n_seq, n_rep, hops,
    tok, gain, direc, ids, ids_t, probs, wg, wu, wd,
    out,
    wbuf, stage, rows, send1, recv1, send2, recv2, hid, comb, unit, moe, part_out, part_in, dot_out, dot_in,
    loc, own, sx, rx, sf, rf, s1, r1, s2, r2, sp, rp, sd, rd,
):
    me = lax.axis_index("seq")
    rep = lax.axis_index("rep")
    tok_rows, width = tok.shape
    n_exp = n_seq
    slots = CAP // n_rep
    cols = width // LANES
    units = wg.shape[0]
    part = width // n_rep
    n_rows = n_exp * slots
    right = lax.rem(rep + 1, n_rep)
    left = lax.rem(rep + n_rep - 1, n_rep)
    far = lax.rem(rep + 2, n_rep)
    weights = (wg, wu, wd)

    def peer_of(i):
        return lax.rem(me + i * hops, n_seq)

    barrier = pltpu.get_barrier_semaphore()

    def greet(i, carry):
        pl.semaphore_signal(barrier, inc=1, device_id=(peer_of(i), rep), device_id_type=MESH)
        return carry

    for k in range(1, n_rep):
        pl.semaphore_signal(
            barrier, inc=1, device_id=(me, lax.rem(rep + k, n_rep)), device_id_type=MESH
        )
    lax.fori_loop(1, n_seq, greet, 0)

    def local_weight(t):
        return pltpu.make_async_copy(weights[t], wbuf.at[t, rep], loc.at[t])

    for t in range(3):
        local_weight(t).start()

    pl.semaphore_wait(barrier, n_seq - 1 + n_rep - 1)

    def direct(t, way):
        return pltpu.make_async_remote_copy(
            src_ref=weights[t],
            dst_ref=wbuf.at[t, rep],
            send_sem=sx.at[t, way],
            recv_sem=rx.at[t, way],
            device_id=(me, (right, left)[way]),
            device_id_type=MESH,
        )

    half = units // 2

    def forward(t, way):
        shard = wbuf.at[t, (left, right)[way], pl.ds(way * half, half)]
        return pltpu.make_async_remote_copy(
            src_ref=shard,
            dst_ref=shard,
            send_sem=sf.at[t, way],
            recv_sem=rf.at[t, way],
            device_id=(me, (right, left)[way]),
            device_id_type=MESH,
        )

    for t in range(2):
        for way in range(2):
            direct(t, way).start()

    tokens = tok[...].astype(F32)
    inv = lax.rsqrt(jnp.mean(tokens * tokens, axis=1, keepdims=True) + 1e-06)
    normed = (tokens * inv * gain[...]).astype(BF16)
    direction = direc[...]
    unit_dir = direction / jnp.sqrt(jnp.sum(direction * direction, axis=1, keepdims=True) + 1e-06)
    unit[...] = unit_dir

    top = ids.shape[1]
    sub = lax.broadcasted_iota(jnp.int32, (n_exp, tok_rows), 0)
    lane = lax.broadcasted_iota(jnp.int32, (n_exp, tok_rows), 1)
    chosen_t = jnp.zeros((n_exp, tok_rows), F32)
    chosen = jnp.zeros((tok_rows, n_exp), F32)
    prob = jnp.zeros((tok_rows, n_exp), F32)
    for k in range(top):
        chosen_t = jnp.where(ids_t[k : k + 1, :] == sub, 1.0, chosen_t)
        same = ids[:, k : k + 1] == lane
        chosen = jnp.where(same, 1.0, chosen)
        prob = jnp.where(same, probs[:, k : k + 1], prob)
    rank_t = dot(chosen_t.astype(BF16), (sub < lane).astype(F32).astype(BF16), ((1,), (0,)))
    rank = dot((lane < sub).astype(F32).astype(BF16), chosen.astype(BF16), ((1,), (0,)))
    first = rep * slots
    rank_t = rank_t.astype(jnp.int32) - first
    rank = rank.astype(jnp.int32) - first
    for c in range(slots):
        pick_t = jnp.where(rank_t == c, chosen_t, 0.0).astype(BF16)
        block = dot(pick_t, normed, ((1,), (0,)))
        for j in range(cols):
            stage[pl.ds(c * cols + j, n_exp, stride=slots * cols), :] = block[
                :, j * LANES : (j + 1) * LANES
            ]
        weight = jnp.where(rank == c, prob, 0.0) * chosen
        high = weight.astype(BF16)
        comb[0:tok_rows, c * n_exp : (c + 1) * n_exp] = high
        comb[tok_rows : 2 * tok_rows, c * n_exp : (c + 1) * n_exp] = (
            weight - high.astype(F32)
        ).astype(BF16)

    step = 8
    message = slots * cols

    def pack(dst):
        def body(b, carry):
            at = pl.multiple_of(b * step, step)
            block = stage[pl.ds(pl.multiple_of(b * (step * message), 16), step * message), :]
            dst[pl.ds(at, step)] = block.astype(BF16).reshape(step, message, LANES)
            return carry

        lax.fori_loop(0, n_exp // step, body, 0)

    def unpack(src):
        def body(b, carry):
            at = pl.multiple_of(b * step, step)
            block = src[pl.ds(at, step)].astype(F32).reshape(step * message, LANES)
            stage[pl.ds(pl.multiple_of(b * (step * message), 16), step * message), :] = block
            return carry

        lax.fori_loop(0, n_exp // step, body, 0)

    def exchange(src, dst, send_sem, recv_sem):
        mine = pltpu.make_async_copy(src.at[me], dst.at[me], own)

        def to(i, carry):
            peer = peer_of(i)
            pltpu.make_async_remote_copy(
                src_ref=src.at[peer],
                dst_ref=dst.at[me],
                send_sem=send_sem,
                recv_sem=recv_sem,
                device_id=(peer, rep),
                device_id_type=MESH,
            ).start()
            return carry

        mine.start()
        lax.fori_loop(1, n_seq, to, 0)
        return mine

    def settle(src, dst, send_sem, recv_sem):
        return pltpu.make_async_remote_copy(
            src_ref=src.at[pl.ds(0, n_seq - 1)],
            dst_ref=dst.at[pl.ds(0, n_seq - 1)],
            send_sem=send_sem,
            recv_sem=recv_sem,
            device_id=(lax.rem(me + 1, n_seq), rep),
            device_id_type=MESH,
        )

    pack(send1)
    mine = exchange(send1, recv1, s1, r1)

    for t in range(2):
        for way in range(2):
            direct(t, way).wait_recv()
            forward(t, way).start()
    for way in range(2):
        direct(2, way).start()

    mine.wait()
    settle(send1, recv1, s1, r1).wait_recv()
    unpack(recv1)
    for j in range(cols):
        rows[:, j * LANES : (j + 1) * LANES] = stage[pl.ds(j, n_rows, stride=cols), :].astype(BF16)

    def gate_up(q):
        x = rows[...]
        g = dot(x, wbuf[0, q], ((1,), (1,)))
        u = dot(x, wbuf[1, q], ((1,), (1,)))
        hid[q] = (g / (1.0 + jnp.exp(-g)) * u).astype(BF16)

    for t in range(3):
        local_weight(t).wait()

    def near(i, carry):
        gate_up(lax.rem(left + i, n_rep))
        return carry

    lax.fori_loop(0, 3, near, 0)
    for way in range(2):
        direct(2, way).wait_recv()
        forward(2, way).start()
    for t in range(2):
        for way in range(2):
            forward(t, way).wait_recv()
    gate_up(far)
    for way in range(2):
        forward(2, way).wait_recv()

    tile = 2 * LANES

    def down(n, carry):
        at = pl.multiple_of(n * tile, tile)
        acc = dot(hid[0], wbuf[2, 0, :, pl.ds(at, tile)], ((1,), (0,)))
        for q in range(1, n_rep):
            acc += dot(hid[q], wbuf[2, q, :, pl.ds(at, tile)], ((1,), (0,)))
        stage[pl.ds(2 * n, n_rows, stride=cols), :] = acc[:, :LANES]
        stage[pl.ds(2 * n + 1, n_rows, stride=cols), :] = acc[:, LANES:]
        return carry

    lax.fori_loop(0, width // tile, down, 0)
    pack(send2)
    mine = exchange(send2, recv2, s2, r2)

    base = jnp.sum(tok[...].astype(F32) * unit[...], axis=1, keepdims=True)

    mine.wait()
    settle(send2, recv2, s2, r2).wait_recv()
    unpack(recv2)
    for c in range(slots):
        for j in range(cols):
            rows[c * n_exp : (c + 1) * n_exp, j * LANES : (j + 1) * LANES] = stage[
                pl.ds(c * cols + j, n_exp, stride=message), :
            ].astype(BF16)
    along = jnp.zeros((tok_rows, 1), F32)
    for q in range(n_rep):
        m = dot(comb[...], rows[:, q * part : (q + 1) * part], ((1,), (0,)))
        m = m[:tok_rows] + m[tok_rows:]
        moe[q] = m
        part_out[q] = m.astype(BF16)
        along += jnp.sum(m * unit[:, q * part : (q + 1) * part], axis=1, keepdims=True)
    dot_out[...] = jnp.broadcast_to(along, (tok_rows, LANES)).T[:8]

    def give(k):
        q = lax.rem(rep + k, n_rep)
        return (
            pltpu.make_async_remote_copy(
                src_ref=part_out.at[q],
                dst_ref=part_in.at[k - 1],
                send_sem=sp.at[k - 1],
                recv_sem=rp.at[k - 1],
                device_id=(me, q),
                device_id_type=MESH,
            ),
            pltpu.make_async_remote_copy(
                src_ref=dot_out,
                dst_ref=dot_in.at[k - 1],
                send_sem=sd.at[k - 1],
                recv_sem=rd.at[k - 1],
                device_id=(me, q),
                device_id_type=MESH,
            ),
        )

    for k in (2, 1, 3):
        for copy in give(k):
            copy.start()
    mine_part = pl.ds(pl.multiple_of(rep * part, part), part)
    residual = tok[:, mine_part].astype(F32) + moe[rep]
    total = dot_out[...]
    for k in range(1, n_rep):
        for copy in give(k):
            copy.wait_recv()
        residual += part_in[k - 1].astype(F32)
        total += dot_in[k - 1]
    total = jnp.broadcast_to(total[0:1], (LANES, tok_rows)).T[:, 0:1] + base
    out[...] = (residual - total * unit[:, mine_part]).astype(BF16)

    for t in range(3):
        for way in range(2):
            direct(t, way).wait_send()
            forward(t, way).wait_send()
    settle(send1, recv1, s1, r1).wait_send()
    settle(send2, recv2, s2, r2).wait_send()
    for k in range(1, n_rep):
        for copy in give(k):
            copy.wait_send()


def local(tokens, norm_gain, refusal_dir, expert_ids, gate_probs, w_gate, w_up, w_down):
    tok_rows, width = tokens.shape
    n_seq = lax.axis_size("seq")
    n_rep = lax.axis_size("rep")
    slots = CAP // n_rep
    units = w_gate.shape[1]
    cols = width // LANES
    message = slots * cols
    part = width // n_rep
    vmem = pl.BlockSpec(memory_space=pltpu.VMEM)
    whole = pl.BlockSpec(memory_space=pl.ANY)
    dma = pltpu.SemaphoreType.DMA
    return pl.pallas_call(
        functools.partial(kernel, n_seq, n_rep, 37 if n_seq > 37 else 1),
        name="moe",
        out_shape=jax.ShapeDtypeStruct((tok_rows, part), BF16),
        in_specs=[vmem] * 6 + [whole] * 3,
        out_specs=vmem,
        scratch_shapes=[
            pltpu.VMEM((3, n_rep, units, width), BF16),
            pltpu.VMEM((n_seq * message, LANES), F32),
            pltpu.VMEM((n_seq * slots, width), BF16),
            pltpu.VMEM((n_seq, message, LANES), BF16),
            pltpu.VMEM((n_seq, message, LANES), BF16),
            pltpu.VMEM((n_seq, message, LANES), BF16),
            pltpu.VMEM((n_seq, message, LANES), BF16),
            pltpu.VMEM((n_rep, n_seq * slots, units), BF16),
            pltpu.VMEM((2 * tok_rows, n_seq * slots), BF16),
            pltpu.VMEM((1, width), F32),
            pltpu.VMEM((n_rep, tok_rows, part), F32),
            pltpu.VMEM((n_rep, tok_rows, part), BF16),
            pltpu.VMEM((n_rep - 1, tok_rows, part), BF16),
            pltpu.VMEM((8, LANES), F32),
            pltpu.VMEM((n_rep - 1, 8, LANES), F32),
            dma((3,)),
            dma,
            dma((3, 2)),
            dma((3, 2)),
            dma((3, 2)),
            dma((3, 2)),
            dma,
            dma,
            dma,
            dma,
            dma((n_rep - 1,)),
            dma((n_rep - 1,)),
            dma((n_rep - 1,)),
            dma((n_rep - 1,)),
        ],
        compiler_params=pltpu.CompilerParams(
            collective_id=0, has_side_effects=True, vmem_limit_bytes=56 * 1024 * 1024
        ),
    )(
        tokens,
        norm_gain[None],
        refusal_dir[None],
        expert_ids,
        expert_ids.T,
        gate_probs,
        w_gate[0],
        w_up[0],
        w_down[0],
    )


def solution(mesh):
    placed = (
        P("seq", None),
        P(),
        P(),
        P("seq", None),
        P("seq", None),
        P("seq", "rep", None),
        P("seq", "rep", None),
        P("seq", "rep", None),
    )
    return jax.shard_map(
        local, mesh=mesh, in_specs=placed, out_specs=P("seq", "rep"), check_vma=False
    )
```

time: 629 us -> 155 us (0.25); the launches traced: 618 us -> 155 us
  waiting for transfers between devices: 273 us -> 0 us
  blocking collectives: 215 us -> 0 us
  Pallas kernels: 0 us -> 151 us
  local copies, waits for them, and re-layouts: 58.8 us -> 3.7 us
  matrix products: 22.5 us -> 0 us
  starting transfers between devices: 19.8 us -> 0 us
  between operations: 14.7 us -> 0.01 us
  other arithmetic: 14.6 us -> 0 us
    all_to_all x1 -> x0, waiting for transfers between devices: 223 us -> none  [local(): lax.all_to_all(pieces, 'seq', split_axis=0, concat_axis=0, tiled=True)]
    all_to_all x1 -> x0, blocking collectives: 209 us -> none  [local(): lax.all_to_all(sendbuf, 'seq', split_axis=0, concat_axis=0, tiled=True)]
    pallas_call x0 -> x1, Pallas kernels: none -> 151 us  [local(): pl.pallas_call(functools.partial(kernel, n_seq, n_rep, 37 if n_seq > 37 e...]
    reduce_scatter x1 -> x0, waiting for transfers between devices: 49.8 us -> none  [local(): lax.psum_scatter(moe_part.astype(jnp.bfloat16), 'rep', scatter_dimension=...]
    dot_general x2 -> x0, matrix products: 22.5 us -> none  [the longest x1 15.3 us: local(): jnp.einsum('secf,efd->secd', hidden, w_down, preferred_element_type=jnp.f...]
    reshape x2 -> x0, local copies, waits for them, and re-layouts: 21.5 us -> none  [the longest x1 10.9 us: local(): returned = returned.reshape(experts * CAP, model_width)]
    all_to_all x1 -> x0, starting transfers between devices: 19.8 us -> none  [local(): lax.all_to_all(pieces, 'seq', split_axis=0, concat_axis=0, tiled=True)]
    gather x1 -> x0, local copies, waits for them, and re-layouts: 12.5 us -> none  [local(): weighted = returned[target].astype(jnp.float32) * probs_flat]
  transfers between devices with their start and end apart: 2 -> 0, of which waited for: 2 -> 0; matrix products, arithmetic and copies ran while one was open for 0% -> 0% of each run, Pallas kernels for 0% -> 0%
where the time goes in v2:
time: 155 us
  Pallas kernels  151 us (97%)
  local copies, waits for them, and re-layouts  3.7 us (2%)
    pallas_call x1, Pallas kernels, local(): pl.pallas_call(functools.partial(kernel, n_seq, n_rep, 37 if n_seq > 37 e...  151 us
    unnamed x7, local copies, waits for them, and re-layouts  3.7 us

profile of v2, /device:TPU:1, one launch (start us, length us, event | category | flops | bytes accessed | tf_op | source)
XLA Modules:
  0.0 154.8 jit_solution(16882251608577042770)
XLA Ops:
  0.0 0.0 copy-start.1
  0.0 0.7 copy-done.1
  0.7 0.0 copy-start
  0.7 0.7 copy.10.probs
  1.4 0.0 copy-done
  1.4 0.7 copy.9.ids
  2.1 151.0 %moe.1 = bf16[128,512]{1,0:T(8,128)(2,1)} custom-call(bf16[128,2048]{1,0:T(8,128)(2,1)} %tok.1, f32[1,2048]{1,0:T(1,128)} %bitcast.10, f32[1,2048]{1,0:T(1,128)} %bitcast.11, s32[128,8]{1,0:T(8,128)} %copy.9.ids, s32[8,128]{1,0:T(8,128)} %bitcast.9, f32[128,8]{1,0:T(8,128)} %copy.10.probs, bf16[192,2048]{1,0:T(8,128)(2,1)} %bitcast.6, ...), custom_call_target="tpu_custom_call" | custom-call | tf_op jit(solution)/shard_map/moe/pallas_call | solution.py:311
  153.2 1.6 %copy.12 = bf16[128,512]{1,0:T(8,128)(2,1)} copy(bf16[128,512]{1,0:T(8,128)(2,1)} %moe.1) | data formatting | bytes 262144
Async XLA Ops:
  0.0 0.7 copy-start.1
  0.7 0.7 copy-start

commit v3 on v2

v3 whole, which is shorter than its diff:
```python
import functools

import jax
import jax.numpy as jnp
from jax import lax
from jax.experimental import pallas as pl
from jax.experimental.pallas import tpu as pltpu
from jax.sharding import PartitionSpec as P

CAP = 12
CHUNKS = 2
LANES = 128
MESH = pl.DeviceIdType.MESH
F32 = jnp.float32
BF16 = jnp.bfloat16


def dot(a, b, dims):
    return lax.dot_general(a, b, (dims, ((), ())), preferred_element_type=F32)


def kernel(
    n_seq, n_rep, hops, group,
    tok, gain, direc, ids_t, probs_t, wg, wu, wd,
    out,
    wbuf, dbuf, stage, rows, send1, recv1, send2, recv2, hid, comb, unit, moe, part_out, part_in, dot_out, dot_in,
    met, loc, loc_d, own, sx, rx, sf, rf, sx_d, rx_d, sf_d, rf_d, s1, r1, s2, r2, sp, rp, sd, rd,
):
    me = lax.axis_index("seq")
    rep = lax.axis_index("rep")
    tok_rows, width = tok.shape
    n_exp = n_seq
    slots = CAP // n_rep
    cols = width // LANES
    units = wg.shape[0]
    part = width // n_rep
    n_rows = n_exp * slots
    chunks = dbuf.shape[0]
    sub = part // chunks
    wide = cols // chunks
    per = sub // LANES
    right = lax.rem(rep + 1, n_rep)
    left = lax.rem(rep + n_rep - 1, n_rep)
    far = lax.rem(rep + 2, n_rep)
    beside = (right, left)

    def peer_of(i):
        return lax.rem(me + i * hops, n_seq)

    n_groups = n_seq // group
    place = lax.rem(me, group)
    first_of = me - place
    barrier = pltpu.get_barrier_semaphore()

    def greet(sem, seq, q):
        pl.semaphore_signal(sem, inc=1, device_id=(seq, q), device_id_type=MESH)

    def greet_group(i, carry):
        greet(barrier, first_of + lax.rem(place + i, group), rep)
        return carry

    def counterpart(i):
        return lax.rem(me + i * group, n_seq)

    def greet_counterpart(i, carry):
        greet(barrier, counterpart(i), rep)
        return carry

    def meet(i, carry):
        greet(met, counterpart(i), rep)
        return carry

    for k in range(1, n_rep):
        greet(barrier, me, lax.rem(rep + k, n_rep))
    lax.fori_loop(1, n_groups, greet_counterpart, 0)
    lax.fori_loop(1, group, greet_group, 0)

    weights = (wg, wu)

    def local_weight(t):
        return pltpu.make_async_copy(weights[t], wbuf.at[t, rep], loc.at[t])

    def down_cols(i, q):
        return wd.at[:, pl.ds(q * part + i * sub, sub)]

    def local_down(i, q):
        return pltpu.make_async_copy(down_cols(i, q), dbuf.at[i, q, rep], loc_d.at[i, q])

    for t in range(2):
        local_weight(t).start()
    for i in range(chunks):
        for q in range(n_rep):
            local_down(i, q).start()

    pl.semaphore_wait(barrier, n_rep - 1 + n_groups - 1 + group - 1)

    half = units // 2

    def pass_on(src, dst, send_sem, recv_sem, way):
        return pltpu.make_async_remote_copy(
            src_ref=src,
            dst_ref=dst,
            send_sem=send_sem,
            recv_sem=recv_sem,
            device_id=(me, beside[way]),
            device_id_type=MESH,
        )

    def direct(t, way):
        return pass_on(weights[t], wbuf.at[t, rep], sx.at[t, way], rx.at[t, way], way)

    def forward(t, way):
        shard = wbuf.at[t, beside[1 - way], pl.ds(way * half, half)]
        return pass_on(shard, shard, sf.at[t, way], rf.at[t, way], way)

    def direct_down(i, q, way):
        return pass_on(
            down_cols(i, q), dbuf.at[i, q, rep], sx_d.at[i, q, way], rx_d.at[i, q, way], way
        )

    def forward_down(i, q, way):
        shard = dbuf.at[i, q, beside[1 - way], pl.ds(way * half, half)]
        return pass_on(shard, shard, sf_d.at[i, q, way], rf_d.at[i, q, way], way)

    ways = range(2)
    quarters = range(n_rep)
    for t in range(2):
        for way in ways:
            direct(t, way).start()

    lax.fori_loop(1, n_groups, meet, 0)

    tokens = tok[...].astype(F32)
    inv = lax.rsqrt(jnp.mean(tokens * tokens, axis=1, keepdims=True) + 1e-06)
    normed = (tokens * inv * gain[...]).astype(BF16)

    top = ids_t.shape[0]
    expert = lax.broadcasted_iota(jnp.int32, (n_exp, tok_rows), 0)
    token = lax.broadcasted_iota(jnp.int32, (n_exp, tok_rows), 1)
    chosen = jnp.zeros((n_exp, tok_rows), F32)
    prob = jnp.zeros((n_exp, tok_rows), F32)
    for k in range(top):
        same = ids_t[k : k + 1, :] == expert
        chosen = jnp.where(same, 1.0, chosen)
        prob = jnp.where(same, probs_t[k : k + 1, :], prob)
    rank = dot(chosen.astype(BF16), (expert < token).astype(F32).astype(BF16), ((1,), (0,)))
    rank = rank.astype(jnp.int32) - rep * slots
    message = slots * cols
    for c in range(slots):
        pick = jnp.where(rank == c, chosen, 0.0).astype(BF16)
        block = dot(pick, normed, ((1,), (0,)))
        for j in range(cols):
            stage[pl.ds(c * cols + j, n_exp, stride=message), :] = block[
                :, j * LANES : (j + 1) * LANES
            ]

    step = 8

    def pack(dst, size):
        def body(b, carry):
            at = pl.multiple_of(b * step, step)
            block = stage[pl.ds(pl.multiple_of(b * (step * size), 16), step * size), :]
            dst[pl.ds(at, step)] = block.astype(BF16).reshape(step, size, LANES)
            return carry

        lax.fori_loop(0, n_exp // step, body, 0)

    def unpack(src, size):
        def body(b, carry):
            at = pl.multiple_of(b * step, step)
            block = src[pl.ds(at, step)].astype(F32).reshape(step * size, LANES)
            stage[pl.ds(pl.multiple_of(b * (step * size), 16), step * size), :] = block
            return carry

        lax.fori_loop(0, n_exp // step, body, 0)

    def keep(src, dst, sem):
        return pltpu.make_async_copy(src.at[me], dst.at[me], sem)

    def exchange(src, dst, send_sem, recv_sem):
        def to(i, carry):
            peer = peer_of(i)
            pltpu.make_async_remote_copy(
                src_ref=src.at[peer],
                dst_ref=dst.at[me],
                send_sem=send_sem,
                recv_sem=recv_sem,
                device_id=(peer, rep),
                device_id_type=MESH,
            ).start()
            return carry

        lax.fori_loop(1, n_seq, to, 0)

    def settle(src, dst, send_sem, recv_sem):
        return pltpu.make_async_remote_copy(
            src_ref=src.at[pl.ds(0, n_seq - 1)],
            dst_ref=dst.at[pl.ds(0, n_seq - 1)],
            send_sem=send_sem,
            recv_sem=recv_sem,
            device_id=(lax.rem(me + 1, n_seq), rep),
            device_id_type=MESH,
        )

    pack(send1, message)
    pl.semaphore_wait(met, n_groups - 1)
    exchange(send1, recv1, s1, r1)
    keep(send1, recv1, own.at[0]).start()

    for t in range(2):
        for way in ways:
            direct(t, way).wait_recv()
            forward(t, way).start()
    for q in quarters:
        for way in ways:
            direct_down(0, q, way).start()

    for c in range(slots):
        weight = (jnp.where(rank == c, prob, 0.0) * chosen).T
        high = weight.astype(BF16)
        comb[0:tok_rows, c * n_exp : (c + 1) * n_exp] = high
        comb[tok_rows : 2 * tok_rows, c * n_exp : (c + 1) * n_exp] = (
            weight - high.astype(F32)
        ).astype(BF16)
    direction = direc[...]
    unit[...] = direction / jnp.sqrt(
        jnp.sum(direction * direction, axis=1, keepdims=True) + 1e-06
    )
    for t in range(2):
        local_weight(t).wait()
    for i in range(chunks):
        for q in quarters:
            local_down(i, q).wait()

    keep(send1, recv1, own.at[0]).wait()
    settle(send1, recv1, s1, r1).wait_recv()
    unpack(recv1, message)
    for j in range(cols):
        rows[:, j * LANES : (j + 1) * LANES] = stage[pl.ds(j, n_rows, stride=cols), :].astype(BF16)

    def gate_up(q):
        x = rows[...]
        g = dot(x, wbuf[0, q], ((1,), (1,)))
        u = dot(x, wbuf[1, q], ((1,), (1,)))
        hid[q] = (g / (1.0 + jnp.exp(-g)) * u).astype(BF16)

    def near(i, carry):
        gate_up(lax.rem(left + i, n_rep))
        return carry

    lax.fori_loop(0, 3, near, 0)
    for q in quarters:
        for way in ways:
            direct_down(0, q, way).wait_recv()
            forward_down(0, q, way).start()
    for t in range(2):
        for way in ways:
            forward(t, way).wait_recv()
    gate_up(far)

    size = slots * wide
    for i in range(chunks):
        for q in quarters:
            for way in ways:
                forward_down(i, q, way).wait_recv()
        if i + 1 < chunks:
            for q in quarters:
                for way in ways:
                    direct_down(i + 1, q, way).start()

        def down(q, carry):
            acc = dot(hid[0], dbuf[i, q, 0], ((1,), (0,)))
            for other in range(1, n_rep):
                acc += dot(hid[other], dbuf[i, q, other], ((1,), (0,)))
            for j in range(per):
                stage[pl.ds(per * q + j, n_rows, stride=wide), :] = acc[
                    :, j * LANES : (j + 1) * LANES
                ]
            return carry

        lax.fori_loop(0, n_rep, down, 0)
        pack(send2.at[i], size)
        exchange(send2.at[i], recv2.at[i], s2.at[i], r2.at[i])
        keep(send2.at[i], recv2.at[i], own.at[1 + i]).start()
        if i + 1 < chunks:
            for q in quarters:
                for way in ways:
                    direct_down(i + 1, q, way).wait_recv()
                    forward_down(i + 1, q, way).start()

    base = jnp.sum(tok[...].astype(F32) * unit[...], axis=1, keepdims=True)

    def give(i, k):
        q = lax.rem(rep + k, n_rep)
        return pltpu.make_async_remote_copy(
            src_ref=part_out.at[i, q],
            dst_ref=part_in.at[i, k - 1],
            send_sem=sp.at[i, k - 1],
            recv_sem=rp.at[i, k - 1],
            device_id=(me, q),
            device_id_type=MESH,
        )

    def give_dot(k):
        return pltpu.make_async_remote_copy(
            src_ref=dot_out,
            dst_ref=dot_in.at[k - 1],
            send_sem=sd.at[k - 1],
            recv_sem=rd.at[k - 1],
            device_id=(me, lax.rem(rep + k, n_rep)),
            device_id_type=MESH,
        )

    along = jnp.zeros((tok_rows, 1), F32)
    for i in range(chunks):
        keep(send2.at[i], recv2.at[i], own.at[1 + i]).wait()
        settle(send2.at[i], recv2.at[i], s2.at[i], r2.at[i]).wait_recv()
        unpack(recv2.at[i], size)
        for c in range(slots):
            for j in range(wide):
                rows[c * n_exp : (c + 1) * n_exp, j * LANES : (j + 1) * LANES] = stage[
                    pl.ds(c * wide + j, n_exp, stride=size), :
                ].astype(BF16)
        for q in quarters:
            m = dot(comb[...], rows[:, q * sub : (q + 1) * sub], ((1,), (0,)))
            m = m[:tok_rows] + m[tok_rows:]
            moe[i, q] = m
            part_out[i, q] = m.astype(BF16)
            at = q * part + i * sub
            along += jnp.sum(m * unit[:, at : at + sub], axis=1, keepdims=True)
        for k in (2, 1, 3):
            give(i, k).start()
    dot_out[...] = jnp.broadcast_to(along, (tok_rows, LANES)).T[:8]
    for k in (2, 1, 3):
        give_dot(k).start()

    total = dot_out[...]
    for k in range(1, n_rep):
        give_dot(k).wait_recv()
        total += dot_in[k - 1]
    total = jnp.broadcast_to(total[0:1], (LANES, tok_rows)).T[:, 0:1] + base
    for i in range(chunks):
        mine = pl.ds(pl.multiple_of(rep * part + i * sub, sub), sub)
        residual = tok[:, mine].astype(F32) + moe[i, rep]
        for k in range(1, n_rep):
            give(i, k).wait_recv()
            residual += part_in[i, k - 1].astype(F32)
        out[:, i * sub : (i + 1) * sub] = (residual - total * unit[:, mine]).astype(BF16)

    for way in ways:
        for t in range(2):
            direct(t, way).wait_send()
            forward(t, way).wait_send()
        for i in range(chunks):
            for q in quarters:
                direct_down(i, q, way).wait_send()
                forward_down(i, q, way).wait_send()
    settle(send1, recv1, s1, r1).wait_send()
    for i in range(chunks):
        settle(send2.at[i], recv2.at[i], s2.at[i], r2.at[i]).wait_send()
        for k in range(1, n_rep):
            give(i, k).wait_send()
    for k in range(1, n_rep):
        give_dot(k).wait_send()


def local(tokens, norm_gain, refusal_dir, expert_ids, gate_probs, w_gate, w_up, w_down):
    tok_rows, width = tokens.shape
    n_seq = lax.axis_size("seq")
    n_rep = lax.axis_size("rep")
    slots = CAP // n_rep
    units = w_gate.shape[1]
    cols = width // LANES
    message = slots * cols
    part = width // n_rep
    sub = part // CHUNKS
    vmem = pl.BlockSpec(memory_space=pltpu.VMEM)
    whole = pl.BlockSpec(memory_space=pl.ANY)
    dma = pltpu.SemaphoreType.DMA
    return pl.pallas_call(
        functools.partial(kernel, n_seq, n_rep, 37, 16),
        name="moe",
        out_shape=jax.ShapeDtypeStruct((tok_rows, part), BF16),
        in_specs=[vmem] * 5 + [whole] * 3,
        out_specs=vmem,
        scratch_shapes=[
            pltpu.VMEM((2, n_rep, units, width), BF16),
            pltpu.VMEM((CHUNKS, n_rep, n_rep, units, sub), BF16),
            pltpu.VMEM((n_seq * message, LANES), F32),
            pltpu.VMEM((n_seq * slots, width), BF16),
            pltpu.VMEM((n_seq, message, LANES), BF16),
            pltpu.VMEM((n_seq, message, LANES), BF16),
            pltpu.VMEM((CHUNKS, n_seq, message // CHUNKS, LANES), BF16),
            pltpu.VMEM((CHUNKS, n_seq, message // CHUNKS, LANES), BF16),
            pltpu.VMEM((n_rep, n_seq * slots, units), BF16),
            pltpu.VMEM((2 * tok_rows, n_seq * slots), BF16),
            pltpu.VMEM((1, width), F32),
            pltpu.VMEM((CHUNKS, n_rep, tok_rows, sub), F32),
            pltpu.VMEM((CHUNKS, n_rep, tok_rows, sub), BF16),
            pltpu.VMEM((CHUNKS, n_rep - 1, tok_rows, sub), BF16),
            pltpu.VMEM((8, LANES), F32),
            pltpu.VMEM((n_rep - 1, 8, LANES), F32),
            pltpu.SemaphoreType.REGULAR,
            dma((2,)),
            dma((CHUNKS, n_rep)),
            dma((1 + CHUNKS,)),
            dma((2, 2)),
            dma((2, 2)),
            dma((2, 2)),
            dma((2, 2)),
            dma((CHUNKS, n_rep, 2)),
            dma((CHUNKS, n_rep, 2)),
            dma((CHUNKS, n_rep, 2)),
            dma((CHUNKS, n_rep, 2)),
            dma,
            dma,
            dma((CHUNKS,)),
            dma((CHUNKS,)),
            dma((CHUNKS, n_rep - 1)),
            dma((CHUNKS, n_rep - 1)),
            dma((n_rep - 1,)),
            dma((n_rep - 1,)),
        ],
        compiler_params=pltpu.CompilerParams(
            collective_id=0, has_side_effects=True, vmem_limit_bytes=56 * 1024 * 1024
        ),
    )(
        tokens,
        norm_gain[None],
        refusal_dir[None],
        expert_ids.T,
        gate_probs.T,
        w_gate[0],
        w_up[0],
        w_down[0],
    )


def solution(mesh):
    placed = (
        P("seq", None),
        P(),
        P(),
        P("seq", None),
        P("seq", None),
        P("seq", "rep", None),
        P("seq", "rep", None),
        P("seq", "rep", None),
    )
    return jax.shard_map(
        local, mesh=mesh, in_specs=placed, out_specs=P("seq", "rep"), check_vma=False
    )
```

time: 155 us -> 130 us (0.84)
  Pallas kernels: 151 us -> 128 us
  local copies, waits for them, and re-layouts: 3.7 us -> 1.57 us
    pallas_call x1, Pallas kernels: 151 us -> 128 us  [local(): pl.pallas_call(functools.partial(kernel, n_seq, n_rep, 37, 16), name='moe...]
    unnamed x7 -> x1, local copies, waits for them, and re-layouts: 3.7 us -> 1.57 us
where the time goes in v3:
time: 130 us
  Pallas kernels  128 us (98%)
  local copies, waits for them, and re-layouts  1.57 us (1%)
    pallas_call x1, Pallas kernels, local(): pl.pallas_call(functools.partial(kernel, n_seq, n_rep, 37, 16), name='moe...  128 us

profile of v3, /device:TPU:1, one launch (start us, length us, event | category | flops | bytes accessed | tf_op | source)
XLA Modules:
  0.0 129.5 jit_solution(5750464464083918464)
XLA Ops:
  0.0 128.0 %moe.1 = bf16[128,512]{1,0:T(8,128)(2,1)} custom-call(bf16[128,2048]{1,0:T(8,128)(2,1)} %tok.1, f32[1,2048]{1,0:T(1,128)} %bitcast.10, f32[1,2048]{1,0:T(1,128)} %bitcast.11, s32[8,128]{1,0:T(8,128)} %bitcast.12, f32[8,128]{1,0:T(8,128)} %bitcast.13, bf16[192,2048]{1,0:T(8,128)(2,1)} %bitcast.7, bf16[192,2048]{1,0:T(8,128)(2,1)} %bitcast.8, ...), custom_call_target="tpu_custom_call" | custom-call | tf_op jit(solution)/shard_map/moe/pallas_call | solution.py:380
  128.0 1.6 %copy.10 = bf16[128,512]{1,0:T(8,128)(2,1)} copy(bf16[128,512]{1,0:T(8,128)(2,1)} %moe.1) | data formatting | bytes 262144

commit v4 on v3

--- a/solution.py
+++ b/solution.py
@@ -49,6 +49,7 @@
 
     n_groups = n_seq // group
     place = lax.rem(me, group)
+    mine_at = me // group
     first_of = me - place
     barrier = pltpu.get_barrier_semaphore()
 
@@ -59,20 +60,24 @@
         greet(barrier, first_of + lax.rem(place + i, group), rep)
         return carry
 
-    def counterpart(i):
-        return lax.rem(me + i * group, n_seq)
-
-    def greet_counterpart(i, carry):
-        greet(barrier, counterpart(i), rep)
-        return carry
-
-    def meet(i, carry):
-        greet(met, counterpart(i), rep)
-        return carry
+    def below(far_by):
+        return (mine_at + n_groups - far_by) // n_groups
+
+    def above(far_by):
+        return (2 * n_groups - 1 - far_by - mine_at) // n_groups
+
+    def greet_line(sem, far_by):
+        @pl.when(below(far_by) == 1)
+        def _():
+            greet(sem, me - far_by * group, rep)
+
+        @pl.when(above(far_by) == 1)
+        def _():
+            greet(sem, me + far_by * group, rep)
 
     for k in range(1, n_rep):
         greet(barrier, me, lax.rem(rep + k, n_rep))
-    lax.fori_loop(1, n_groups, greet_counterpart, 0)
+    greet_line(barrier, 1)
     lax.fori_loop(1, group, greet_group, 0)
 
     weights = (wg, wu)
@@ -92,7 +97,7 @@
         for q in range(n_rep):
             local_down(i, q).start()
 
-    pl.semaphore_wait(barrier, n_rep - 1 + n_groups - 1 + group - 1)
+    pl.semaphore_wait(barrier, n_rep - 1 + group - 1 + below(1) + above(1))
 
     half = units // 2
 
@@ -128,7 +133,7 @@
         for way in ways:
             direct(t, way).start()
 
-    lax.fori_loop(1, n_groups, meet, 0)
+    greet_line(met.at[0], 1)
 
     tokens = tok[...].astype(F32)
     inv = lax.rsqrt(jnp.mean(tokens * tokens, axis=1, keepdims=True) + 1e-06)
@@ -203,7 +208,10 @@
         )
 
     pack(send1, message)
-    pl.semaphore_wait(met, n_groups - 1)
+    for at, far_by in enumerate((1, 2, 4)):
+        if at:
+            greet_line(met.at[at], far_by)
+        pl.semaphore_wait(met.at[at], below(far_by) + above(far_by))
     exchange(send1, recv1, s1, r1)
     keep(send1, recv1, own.at[0]).start()
 
@@ -400,7 +408,7 @@
             pltpu.VMEM((CHUNKS, n_rep - 1, tok_rows, sub), BF16),
             pltpu.VMEM((8, LANES), F32),
             pltpu.VMEM((n_rep - 1, 8, LANES), F32),
-            pltpu.SemaphoreType.REGULAR,
+            pltpu.SemaphoreType.REGULAR((3,)),
             dma((2,)),
             dma((CHUNKS, n_rep)),
             dma((1 + CHUNKS,)),

time: 130 us -> 130 us (level)
  no operation moved by 1% of the time
where the time goes in v4:
time: 130 us
  Pallas kernels  128 us (98%)
  local copies, waits for them, and re-layouts  1.57 us (1%)
    pallas_call x1, Pallas kernels, local(): pl.pallas_call(functools.partial(kernel, n_seq, n_rep, 37, 16), name='moe...  128 us

profile of v4, /device:TPU:1, one launch (start us, length us, event | category | flops | bytes accessed | tf_op | source)
XLA Modules:
  0.0 129.6 jit_solution(9233672262104627211)
XLA Ops:
  0.0 128.0 %moe.1 = bf16[128,512]{1,0:T(8,128)(2,1)} custom-call(bf16[128,2048]{1,0:T(8,128)(2,1)} %tok.1, f32[1,2048]{1,0:T(1,128)} %bitcast.10, f32[1,2048]{1,0:T(1,128)} %bitcast.11, s32[8,128]{1,0:T(8,128)} %bitcast.12, f32[8,128]{1,0:T(8,128)} %bitcast.13, bf16[192,2048]{1,0:T(8,128)(2,1)} %bitcast.7, bf16[192,2048]{1,0:T(8,128)(2,1)} %bitcast.8, ...), custom_call_target="tpu_custom_call" | custom-call | tf_op jit(solution)/shard_map/moe/pallas_call | solution.py:388
  128.0 1.6 %copy.10 = bf16[128,512]{1,0:T(8,128)(2,1)} copy(bf16[128,512]{1,0:T(8,128)(2,1)} %moe.1) | data formatting | bytes 262144

commit v5 on v4

--- a/solution.py
+++ b/solution.py
@@ -47,6 +47,9 @@
     def peer_of(i):
         return lax.rem(me + i * hops, n_seq)
 
+    def source_of(i):
+        return lax.rem(me + (n_seq - i) * hops, n_seq)
+
     n_groups = n_seq // group
     place = lax.rem(me, group)
     mine_at = me // group
@@ -85,17 +88,27 @@
     def local_weight(t):
         return pltpu.make_async_copy(weights[t], wbuf.at[t, rep], loc.at[t])
 
-    def down_cols(i, q):
-        return wd.at[:, pl.ds(q * part + i * sub, sub)]
-
-    def local_down(i, q):
-        return pltpu.make_async_copy(down_cols(i, q), dbuf.at[i, q, rep], loc_d.at[i, q])
+    steps = (
+        ((0, 0, 0, sub), (0, 1, 0, LANES)),
+        ((0, 1, LANES, sub - LANES), (0, 2, 0, sub), (0, 3, 0, sub)),
+        tuple((1, q, 0, sub) for q in range(n_rep)),
+    )
+    pieces = sum(steps, ())
+
+    def down_cols(p):
+        i, q, lo, n = p
+        return wd.at[:, pl.ds(q * part + i * sub + lo, n)]
+
+    def local_down(p):
+        i, q, lo, n = p
+        return pltpu.make_async_copy(
+            down_cols(p), dbuf.at[i, q, rep, :, pl.ds(lo, n)], loc_d.at[pieces.index(p)]
+        )
 
     for t in range(2):
         local_weight(t).start()
-    for i in range(chunks):
-        for q in range(n_rep):
-            local_down(i, q).start()
+    for p in pieces:
+        local_down(p).start()
 
     pl.semaphore_wait(barrier, n_rep - 1 + group - 1 + below(1) + above(1))
 
@@ -118,14 +131,22 @@
         shard = wbuf.at[t, beside[1 - way], pl.ds(way * half, half)]
         return pass_on(shard, shard, sf.at[t, way], rf.at[t, way], way)
 
-    def direct_down(i, q, way):
+    def direct_down(p, way):
+        i, q, lo, n = p
+        at = pieces.index(p)
         return pass_on(
-            down_cols(i, q), dbuf.at[i, q, rep], sx_d.at[i, q, way], rx_d.at[i, q, way], way
-        )
-
-    def forward_down(i, q, way):
-        shard = dbuf.at[i, q, beside[1 - way], pl.ds(way * half, half)]
-        return pass_on(shard, shard, sf_d.at[i, q, way], rf_d.at[i, q, way], way)
+            down_cols(p),
+            dbuf.at[i, q, rep, :, pl.ds(lo, n)],
+            sx_d.at[at, way],
+            rx_d.at[at, way],
+            way,
+        )
+
+    def forward_down(p, way):
+        i, q, lo, n = p
+        at = pieces.index(p)
+        shard = dbuf.at[i, q, beside[1 - way], pl.ds(way * half, half), pl.ds(lo, n)]
+        return pass_on(shard, shard, sf_d.at[at, way], rf_d.at[at, way], way)
 
     ways = range(2)
     quarters = range(n_rep)
@@ -160,68 +181,61 @@
             ]
 
     step = 8
-
-    def pack(dst, size):
-        def body(b, carry):
-            at = pl.multiple_of(b * step, step)
-            block = stage[pl.ds(pl.multiple_of(b * (step * size), 16), step * size), :]
-            dst[pl.ds(at, step)] = block.astype(BF16).reshape(step, size, LANES)
-            return carry
-
-        lax.fori_loop(0, n_exp // step, body, 0)
-
-    def unpack(src, size):
-        def body(b, carry):
-            at = pl.multiple_of(b * step, step)
-            block = src[pl.ds(at, step)].astype(F32).reshape(step * size, LANES)
-            stage[pl.ds(pl.multiple_of(b * (step * size), 16), step * size), :] = block
-            return carry
-
-        lax.fori_loop(0, n_exp // step, body, 0)
-
-    def keep(src, dst, sem):
-        return pltpu.make_async_copy(src.at[me], dst.at[me], sem)
-
-    def exchange(src, dst, send_sem, recv_sem):
-        def to(i, carry):
-            peer = peer_of(i)
-            pltpu.make_async_remote_copy(
-                src_ref=src.at[peer],
-                dst_ref=dst.at[me],
-                send_sem=send_sem,
-                recv_sem=recv_sem,
-                device_id=(peer, rep),
-                device_id_type=MESH,
-            ).start()
-            return carry
-
-        lax.fori_loop(1, n_seq, to, 0)
-
-    def settle(src, dst, send_sem, recv_sem):
-        return pltpu.make_async_remote_copy(
-            src_ref=src.at[pl.ds(0, n_seq - 1)],
-            dst_ref=dst.at[pl.ds(0, n_seq - 1)],
-            send_sem=send_sem,
-            recv_sem=recv_sem,
-            device_id=(lax.rem(me + 1, n_seq), rep),
-            device_id_type=MESH,
-        )
-
-    pack(send1, message)
+    block_rows = step * message
+
+    def pack1(b, carry):
+        block = stage[pl.ds(pl.multiple_of(b * block_rows, 16), block_rows), :]
+        send1[pl.ds(b * step, step)] = block.astype(BF16).reshape(step, message, LANES)
+        return carry
+
+    lax.fori_loop(0, n_exp // step, pack1, 0)
+
     for at, far_by in enumerate((1, 2, 4)):
         if at:
             greet_line(met.at[at], far_by)
         pl.semaphore_wait(met.at[at], below(far_by) + above(far_by))
-    exchange(send1, recv1, s1, r1)
-    keep(send1, recv1, own.at[0]).start()
+
+    span = n_seq // 2
+
+    def rows_out(i, h):
+        peer = peer_of(i)
+        return pltpu.make_async_remote_copy(
+            src_ref=send1.at[peer],
+            dst_ref=recv1.at[i],
+            send_sem=s1.at[h],
+            recv_sem=r1.at[h],
+            device_id=(peer, rep),
+            device_id_type=MESH,
+        )
+
+    def rows_all(h):
+        held = pl.ds(0, span - 1 + h)
+        return pltpu.make_async_remote_copy(
+            src_ref=send1.at[held],
+            dst_ref=recv1.at[held],
+            send_sem=s1.at[h],
+            recv_sem=r1.at[h],
+            device_id=(lax.rem(me + 1, n_seq), rep),
+            device_id_type=MESH,
+        )
+
+    own_rows = pltpu.make_async_copy(send1.at[me], recv1.at[0], own.at[0])
+    for h in range(2):
+
+        def rows_to(i, carry):
+            rows_out(i, h).start()
+            return carry
+
+        lax.fori_loop(1 - h + h * span, span + h * span, rows_to, 0)
+    own_rows.start()
 
     for t in range(2):
         for way in ways:
             direct(t, way).wait_recv()
             forward(t, way).start()
-    for q in quarters:
+    for p in steps[0]:
         for way in ways:
-            direct_down(0, q, way).start()
+            direct_down(p, way).start()
 
     for c in range(slots):
         weight = (jnp.where(rank == c, prob, 0.0) * chosen).T
@@ -236,65 +250,133 @@
     )
     for t in range(2):
         local_weight(t).wait()
-    for i in range(chunks):
-        for q in quarters:
-            local_down(i, q).wait()
-
-    keep(send1, recv1, own.at[0]).wait()
-    settle(send1, recv1, s1, r1).wait_recv()
-    unpack(recv1, message)
-    for j in range(cols):
-        rows[:, j * LANES : (j + 1) * LANES] = stage[pl.ds(j, n_rows, stride=cols), :].astype(BF16)
-
-    def gate_up(q):
-        x = rows[...]
+    for p in pieces:
+        local_down(p).wait()
+
+    own_rows.wait()
+    held = span * slots
+
+    def gate_up(q, h):
+        at = pl.ds(h * held, held)
+        x = rows[at, :]
         g = dot(x, wbuf[0, q], ((1,), (1,)))
         u = dot(x, wbuf[1, q], ((1,), (1,)))
-        hid[q] = (g / (1.0 + jnp.exp(-g)) * u).astype(BF16)
-
-    def near(i, carry):
-        gate_up(lax.rem(left + i, n_rep))
-        return carry
-
-    lax.fori_loop(0, 3, near, 0)
-    for q in quarters:
-        for way in ways:
-            direct_down(0, q, way).wait_recv()
-            forward_down(0, q, way).start()
+        hid[q, at, :] = (g / (1.0 + jnp.exp(-g)) * u).astype(BF16)
+
+    for h in range(2):
+        rows_all(h).wait_recv()
+
+        def unpack1(b, carry):
+            at = h * span + b * step
+            block = recv1[pl.ds(at, step)].astype(F32).reshape(block_rows, LANES)
+            stage[pl.ds(pl.multiple_of(at * message, 16), block_rows), :] = block
+            return carry
+
+        lax.fori_loop(0, span // step, unpack1, 0)
+        for c in range(slots):
+            for j in range(cols):
+                rows[h * held + c * span : h * held + (c + 1) * span, j * LANES : (j + 1) * LANES] = (
+                    stage[pl.ds(h * span * message + c * cols + j, span, stride=message), :]
+                ).astype(BF16)
+
+        def near(i, carry):
+            gate_up(lax.rem(left + i, n_rep), h)
+            return carry
+
+        lax.fori_loop(0, 3, near, 0)
+
+    def hand_on(k):
+        for p in steps[k]:
+            for way in ways:
+                direct_down(p, way).wait_recv()
+                forward_down(p, way).start()
+        if k + 1 < len(steps):
+            for p in steps[k + 1]:
+                for way in ways:
+                    direct_down(p, way).start()
+
+    hand_on(0)
     for t in range(2):
         for way in ways:
             forward(t, way).wait_recv()
-    gate_up(far)
+    for h in range(2):
+        gate_up(far, h)
 
     size = slots * wide
-    for i in range(chunks):
-        for q in quarters:
+    returns = ((0, 0, 8), (0, 8, size - 8), (1, 0, size))
+
+    def down(i, q, lo, n):
+        acc = dot(hid[0], dbuf[i, q, 0, :, lo : lo + n], ((1,), (0,)))
+        for other in range(1, n_rep):
+            acc += dot(hid[other], dbuf[i, q, other, :, lo : lo + n], ((1,), (0,)))
+        for j in range(n // LANES):
+            for h in range(2):
+                for c in range(slots):
+                    at = h * held + c * span
+                    to = h * span * size + (per * q + lo // LANES + j) * slots + c
+                    stage[pl.ds(to, span, stride=size), :] = acc[
+                        at : at + span, j * LANES : (j + 1) * LANES
+                    ]
+
+    def back(k, i):
+        chunk, lo, n = returns[k]
+        at = pl.ds(lo, n)
+        return pltpu.make_async_remote_copy(
+            src_ref=send2.at[chunk, i, at],
+            dst_ref=recv2.at[chunk, me, at],
+            send_sem=s2.at[k],
+            recv_sem=r2.at[k],
+            device_id=(source_of(i), rep),
+            device_id_type=MESH,
+        )
+
+    def back_all(k):
+        chunk, lo, n = returns[k]
+        most = pl.ds(0, n_seq - 1)
+        return pltpu.make_async_remote_copy(
+            src_ref=send2.at[chunk, most, pl.ds(lo, n)],
+            dst_ref=recv2.at[chunk, most, pl.ds(lo, n)],
+            send_sem=s2.at[k],
+            recv_sem=r2.at[k],
+            device_id=(lax.rem(me + 1, n_seq), rep),
+            device_id_type=MESH,
+        )
+
+    def back_own(k):
+        chunk, lo, n = returns[k]
+        at = pl.ds(lo, n)
+        return pltpu.make_async_copy(
+            send2.at[chunk, 0, at], recv2.at[chunk, me, at], own.at[1 + k]
+        )
+
+    for k in range(len(steps)):
+        chunk, lo, n = returns[k]
+        for p in steps[k]:
             for way in ways:
-                forward_down(i, q, way).wait_recv()
-        if i + 1 < chunks:
-            for q in quarters:
-                for way in ways:
-                    direct_down(i + 1, q, way).start()
-
-        def down(q, carry):
-            acc = dot(hid[0], dbuf[i, q, 0], ((1,), (0,)))
-            for other in range(1, n_rep):
-                acc += dot(hid[other], dbuf[i, q, other], ((1,), (0,)))
-            for j in range(per):
-                stage[pl.ds(per * q + j, n_rows, stride=wide), :] = acc[
-                    :, j * LANES : (j + 1) * LANES
-                ]
+                forward_down(p, way).wait_recv()
+        if k < 2:
+            for p in steps[k]:
+                down(*p)
+        else:
+            lax.fori_loop(0, n_rep, lambda q, carry: (down(1, q, 0, sub), carry)[1], 0)
+
+        def pack2(b, carry):
+            for u in range(step):
+                i = b * step + u
+                block = stage[pl.ds(pl.multiple_of(i * size + lo, 8), n), :]
+                send2[chunk, i, lo : lo + n, :] = block.astype(BF16)
             return carry
 
-        lax.fori_loop(0, n_rep, down, 0)
-        pack(send2.at[i], size)
-        exchange(send2.at[i], recv2.at[i], s2.at[i], r2.at[i])
-        keep(send2.at[i], recv2.at[i], own.at[1 + i]).start()
-        if i + 1 < chunks:
-            for q in quarters:
-                for way in ways:
-                    direct_down(i + 1, q, way).wait_recv()
-                    forward_down(i + 1, q, way).start()
+        lax.fori_loop(0, n_seq // step, pack2, 0)
+
+        def back_to(i, carry):
+            back(k, i).start()
+            return carry
+
+        lax.fori_loop(1, n_seq, back_to, 0)
+        back_own(k).start()
+        if k + 1 < len(steps):
+            hand_on(k + 1)
 
     base = jnp.sum(tok[...].astype(F32) * unit[...], axis=1, keepdims=True)
 
@@ -321,13 +403,21 @@
 
     along = jnp.zeros((tok_rows, 1), F32)
     for i in range(chunks):
-        keep(send2.at[i], recv2.at[i], own.at[1 + i]).wait()
-        settle(send2.at[i], recv2.at[i], s2.at[i], r2.at[i]).wait_recv()
-        unpack(recv2.at[i], size)
+        for k in range(len(returns)):
+            if returns[k][0] == i:
+                back_own(k).wait()
+                back_all(k).wait_recv()
+
+        def unpack2(b, carry):
+            block = recv2[i, pl.ds(b * step, step)].astype(F32).reshape(step * size, LANES)
+            stage[pl.ds(pl.multiple_of(b * (step * size), 16), step * size), :] = block
+            return carry
+
+        lax.fori_loop(0, n_exp // step, unpack2, 0)
         for c in range(slots):
             for j in range(wide):
                 rows[c * n_exp : (c + 1) * n_exp, j * LANES : (j + 1) * LANES] = stage[
-                    pl.ds(c * wide + j, n_exp, stride=size), :
+                    pl.ds(j * slots + c, n_exp, stride=size), :
                 ].astype(BF16)
         for q in quarters:
             m = dot(comb[...], rows[:, q * sub : (q + 1) * sub], ((1,), (0,)))
@@ -359,13 +449,14 @@
         for t in range(2):
             direct(t, way).wait_send()
             forward(t, way).wait_send()
-        for i in range(chunks):
-            for q in quarters:
-                direct_down(i, q, way).wait_send()
-                forward_down(i, q, way).wait_send()
-    settle(send1, recv1, s1, r1).wait_send()
+        for p in pieces:
+            direct_down(p, way).wait_send()
+            forward_down(p, way).wait_send()
+    for h in range(2):
+        rows_all(h).wait_send()
+    for k in range(len(returns)):
+        back_all(k).wait_send()
     for i in range(chunks):
-        settle(send2.at[i], recv2.at[i], s2.at[i], r2.at[i]).wait_send()
         for k in range(1, n_rep):
             give(i, k).wait_send()
     for k in range(1, n_rep):
@@ -410,20 +501,20 @@
             pltpu.VMEM((n_rep - 1, 8, LANES), F32),
             pltpu.SemaphoreType.REGULAR((3,)),
             dma((2,)),
-            dma((CHUNKS, n_rep)),
-            dma((1 + CHUNKS,)),
+            dma((9,)),
+            dma((4,)),
             dma((2, 2)),
             dma((2, 2)),
             dma((2, 2)),
             dma((2, 2)),
-            dma((CHUNKS, n_rep, 2)),
-            dma((CHUNKS, n_rep, 2)),
-            dma((CHUNKS, n_rep, 2)),
-            dma((CHUNKS, n_rep, 2)),
-            dma,
-            dma,
-            dma((CHUNKS,)),
-            dma((CHUNKS,)),
+            dma((9, 2)),
+            dma((9, 2)),
+            dma((9, 2)),
+            dma((9, 2)),
+            dma((2,)),
+            dma((2,)),
+            dma((3,)),
+            dma((3,)),
             dma((CHUNKS, n_rep - 1)),
             dma((CHUNKS, n_rep - 1)),
             dma((n_rep - 1,)),

time: 130 us -> 127 us (0.977)
  Pallas kernels: 128 us -> 125 us
    pallas_call x1, Pallas kernels: 128 us -> 125 us  [local(): pl.pallas_call(functools.partial(kernel, n_seq, n_rep, 37, 16), name='moe...]
where the time goes in v5:
time: 127 us
  Pallas kernels  125 us (98%)
  local copies, waits for them, and re-layouts  1.57 us (1%)
    pallas_call x1, Pallas kernels, local(): pl.pallas_call(functools.partial(kernel, n_seq, n_rep, 37, 16), name='moe...  125 us

profile of v5, /device:TPU:1, one launch (start us, length us, event | category | flops | bytes accessed | tf_op | source)
XLA Modules:
  0.0 126.9 jit_solution(18077021236093697957)
XLA Ops:
  0.0 125.3 %moe.1 = bf16[128,512]{1,0:T(8,128)(2,1)} custom-call(bf16[128,2048]{1,0:T(8,128)(2,1)} %tok.1, f32[1,2048]{1,0:T(1,128)} %bitcast.10, f32[1,2048]{1,0:T(1,128)} %bitcast.11, s32[8,128]{1,0:T(8,128)} %bitcast.12, f32[8,128]{1,0:T(8,128)} %bitcast.13, bf16[192,2048]{1,0:T(8,128)(2,1)} %bitcast.7, bf16[192,2048]{1,0:T(8,128)(2,1)} %bitcast.8, ...), custom_call_target="tpu_custom_call" | custom-call | tf_op jit(solution)/shard_map/moe/pallas_call | solution.py:479
  125.3 1.6 %copy.10 = bf16[128,512]{1,0:T(8,128)(2,1)} copy(bf16[128,512]{1,0:T(8,128)(2,1)} %moe.1) | data formatting | bytes 262144

commit v6 on v5

--- a/solution.py
+++ b/solution.py
@@ -91,7 +91,8 @@
     steps = (
         ((0, 0, 0, sub), (0, 1, 0, LANES)),
         ((0, 1, LANES, sub - LANES), (0, 2, 0, sub), (0, 3, 0, sub)),
-        tuple((1, q, 0, sub) for q in range(n_rep)),
+        tuple((1, q, 0, sub) for q in range(n_rep - 1)),
+        ((1, n_rep - 1, 0, sub),),
     )
     pieces = sum(steps, ())
 
@@ -263,6 +264,17 @@
         u = dot(x, wbuf[1, q], ((1,), (1,)))
         hid[q, at, :] = (g / (1.0 + jnp.exp(-g)) * u).astype(BF16)
 
+    def send_down(k):
+        for p in steps[k]:
+            for way in ways:
+                direct_down(p, way).start()
+
+    def hand_on(k):
+        for p in steps[k]:
+            for way in ways:
+                direct_down(p, way).wait_recv()
+                forward_down(p, way).start()
+
     for h in range(2):
         rows_all(h).wait_recv()
 
@@ -284,26 +296,18 @@
             return carry
 
         lax.fori_loop(0, 3, near, 0)
-
-    def hand_on(k):
-        for p in steps[k]:
-            for way in ways:
-                direct_down(p, way).wait_recv()
-                forward_down(p, way).start()
-        if k + 1 < len(steps):
-            for p in steps[k + 1]:
-                for way in ways:
-                    direct_down(p, way).start()
-
-    hand_on(0)
+        if h == 0:
+            hand_on(0)
+
     for t in range(2):
         for way in ways:
             forward(t, way).wait_recv()
+    send_down(1)
     for h in range(2):
         gate_up(far, h)
 
     size = slots * wide
-    returns = ((0, 0, 8), (0, 8, size - 8), (1, 0, size))
+    returns = ((0, 0, 8), (0, 8, size - 8), (1, 0, size - 8), (1, size - 8, 8))
 
     def down(i, q, lo, n):
         acc = dot(hid[0], dbuf[i, q, 0, :, lo : lo + n], ((1,), (0,)))
@@ -354,11 +358,8 @@
         for p in steps[k]:
             for way in ways:
                 forward_down(p, way).wait_recv()
-        if k < 2:
-            for p in steps[k]:
-                down(*p)
-        else:
-            lax.fori_loop(0, n_rep, lambda q, carry: (down(1, q, 0, sub), carry)[1], 0)
+        for p in steps[k]:
+            down(*p)
 
         def pack2(b, carry):
             for u in range(step):
@@ -373,10 +374,13 @@
             back(k, i).start()
             return carry
 
-        lax.fori_loop(1, n_seq, back_to, 0)
-        back_own(k).start()
+        lax.fori_loop(1, span, back_to, 0)
         if k + 1 < len(steps):
             hand_on(k + 1)
+        if k + 2 < len(steps):
+            send_down(k + 2)
+        lax.fori_loop(span, n_seq, back_to, 0)
+        back_own(k).start()
 
     base = jnp.sum(tok[...].astype(F32) * unit[...], axis=1, keepdims=True)
 
@@ -402,24 +406,33 @@
         )
 
     along = jnp.zeros((tok_rows, 1), F32)
-    for i in range(chunks):
-        for k in range(len(returns)):
-            if returns[k][0] == i:
-                back_own(k).wait()
-                back_all(k).wait_recv()
-
-        def unpack2(b, carry):
-            block = recv2[i, pl.ds(b * step, step)].astype(F32).reshape(step * size, LANES)
-            stage[pl.ds(pl.multiple_of(b * (step * size), 16), step * size), :] = block
+
+    def landed(i, lo, n):
+        def body(b, carry):
+            block = recv2[i, pl.ds(b * step, step), lo : lo + n, :].astype(F32)
+            stage[pl.ds(pl.multiple_of(b * (step * n), 16), step * n), :] = block.reshape(
+                step * n, LANES
+            )
             return carry
 
-        lax.fori_loop(0, n_exp // step, unpack2, 0)
-        for c in range(slots):
-            for j in range(wide):
+        lax.fori_loop(0, n_exp // step, body, 0)
+
+    landings = (
+        (0, (0, 1), 0, size, range(n_rep)),
+        (1, (2,), 0, size - 8, range(n_rep // 2)),
+        (1, (3,), 8, size - 8, range(n_rep // 2, n_rep)),
+    )
+    for i, waits, lo, n, done in landings:
+        for k in waits:
+            back_own(k).wait()
+            back_all(k).wait_recv()
+        landed(i, lo, n)
+        for j in range(per * done[0], per * done[-1] + per):
+            for c in range(slots):
                 rows[c * n_exp : (c + 1) * n_exp, j * LANES : (j + 1) * LANES] = stage[
-                    pl.ds(j * slots + c, n_exp, stride=size), :
+                    pl.ds(j * slots + c - lo, n_exp, stride=n), :
                 ].astype(BF16)
-        for q in quarters:
+        for q in done:
             m = dot(comb[...], rows[:, q * sub : (q + 1) * sub], ((1,), (0,)))
             m = m[:tok_rows] + m[tok_rows:]
             moe[i, q] = m
@@ -427,7 +440,14 @@
             at = q * part + i * sub
             along += jnp.sum(m * unit[:, at : at + sub], axis=1, keepdims=True)
         for k in (2, 1, 3):
-            give(i, k).start()
+            if len(done) == n_rep:
+                give(i, k).start()
+            else:
+
+                @pl.when(lax.rem(rep + k, n_rep) // len(done) == done[0] // len(done))
+                def _():
+                    give(i, k).start()
+
     dot_out[...] = jnp.broadcast_to(along, (tok_rows, LANES)).T[:8]
     for k in (2, 1, 3):
         give_dot(k).start()
@@ -502,7 +522,7 @@
             pltpu.SemaphoreType.REGULAR((3,)),
             dma((2,)),
             dma((9,)),
-            dma((4,)),
+            dma((5,)),
             dma((2, 2)),
             dma((2, 2)),
             dma((2, 2)),
@@ -513,8 +533,8 @@
             dma((9, 2)),
             dma((2,)),
             dma((2,)),
-            dma((3,)),
-            dma((3,)),
+            dma((4,)),
+            dma((4,)),
             dma((CHUNKS, n_rep - 1)),
             dma((CHUNKS, n_rep - 1)),
             dma((n_rep - 1,)),

time: 127 us -> 126 us (level)
  no operation moved by 1% of the time
where the time goes in v6:
time: 126 us
  Pallas kernels  125 us (99%)
  local copies, waits for them, and re-layouts  1.57 us (1%)
    pallas_call x1, Pallas kernels, local(): pl.pallas_call(functools.partial(kernel, n_seq, n_rep, 37, 16), name='moe...  125 us

profile of v6, /device:TPU:1, one launch (start us, length us, event | category | flops | bytes accessed | tf_op | source)
XLA Modules:
  0.0 126.2 jit_solution(16001123613989041813)
XLA Ops:
  0.0 124.6 %moe.1 = bf16[128,512]{1,0:T(8,128)(2,1)} custom-call(bf16[128,2048]{1,0:T(8,128)(2,1)} %tok.1, f32[1,2048]{1,0:T(1,128)} %bitcast.10, f32[1,2048]{1,0:T(1,128)} %bitcast.11, s32[8,128]{1,0:T(8,128)} %bitcast.12, f32[8,128]{1,0:T(8,128)} %bitcast.13, bf16[192,2048]{1,0:T(8,128)(2,1)} %bitcast.7, bf16[192,2048]{1,0:T(8,128)(2,1)} %bitcast.8, ...), custom_call_target="tpu_custom_call" | custom-call | tf_op jit(solution)/shard_map/moe/pallas_call | solution.py:499
  124.6 1.6 %copy.10 = bf16[128,512]{1,0:T(8,128)(2,1)} copy(bf16[128,512]{1,0:T(8,128)(2,1)} %moe.1) | data formatting | bytes 262144
